TPU v7x, 768 devices: a whole 4x8x12 slice. The times are simulated.
768 devices in a mesh: dp: 96 (over y, z_lo, core), ctx: 8 (over x, z_hi).
Axes of the slice: x: 4, y: 8, z: 12 (z_hi: 2, z_lo: 6; z = z_hi * 6 + z_lo), core: 2. Of those that a mesh axis runs over, the one named last changes fastest.
Arguments:
- inputs: bfloat16 [96, 1024, 9216], P('dp', 'ctx'), may hold values from -6 to 6
- block_order: int32 [16], replicated, may hold values from 0 to 15, each once
- w_value: bfloat16 [9216, 128], P('dp'), may hold values from -0.0625 to 0.0625
- query: bfloat16 [96, 1024, 2048], P('dp', 'ctx'), may hold values from -6 to 6
- keys: bfloat16 [96, 1024, 128], P('dp', 'ctx'), may hold values from -6 to 6
- out_grad: bfloat16 [96, 1024, 2048], P('dp', 'ctx'), may hold values from -6 to 6
Outputs:
- attn_out: bfloat16 [96, 1024, 2048], P('dp', 'ctx')
- grad_query: bfloat16 [96, 1024, 2048], P('dp', 'ctx')
- grad_keys: bfloat16 [96, 1024, 128], P('dp', 'ctx')
- grad_w: float32 [9216, 128], P('dp')
Inputs may be any that keep to these rules, and one draw needn't show every extreme that they name: `block_order`: a permutation of the block numbers.
All inputs are finite; a program needn't handle non-finite values.
Results may differ from a plain program's by a relative error of at most 0.02.
Values may be sent and summed in bfloat16 or wider, within the bound.
No kernel may reach another device: no remote copies, remote signals or barrier semaphores. Data moves between devices by JAX's collectives and lax.ppermute only.
A program may use at most 64 MiB of HBM per device.

v0:
```python
import jax
import jax.numpy as jnp
from jax import lax
from jax.sharding import PartitionSpec as P

BLK = 64


def shifted(value, axis, steps):
    count = lax.axis_size(axis)
    pairs = [(source, (source + steps) % count) for source in range(count)]
    return lax.ppermute(value, axis, pairs)


def shards(inputs, block_order, w_value, query, keys, out_grad):
    x_rows = inputs[0]
    q_rows = query[0]
    k_rows = keys[0]
    grad_rows = out_grad[0]
    rows = x_rows.shape[0]
    head_size = k_rows.shape[1]
    head_count = q_rows.shape[1] // head_size
    scale = 1.0 / head_size**0.5
    values = jnp.dot(
        x_rows,
        lax.all_gather(w_value, "dp", axis=0, tiled=True),
        preferred_element_type=jnp.float32,
    ).astype(jnp.bfloat16)
    far_keys, far_values = shifted((k_rows, values), "ctx", 1)
    index = lax.axis_index("ctx")
    count = lax.axis_size("ctx")
    before = (index + count - 1) % count
    local_iota = jnp.arange(rows, dtype=jnp.int32)

    def places(owner):
        slots = lax.dynamic_slice_in_dim(block_order, 2 * owner, 2, 0)
        return slots[local_iota // BLK] * BLK + local_iota % BLK

    mine = places(index)
    theirs = places(before)
    key_place = jnp.concatenate([mine, theirs], axis=0)
    allowed = key_place[None, :] <= mine[:, None]
    all_keys = jnp.concatenate([k_rows, far_keys], axis=0)
    all_values = jnp.concatenate([values, far_values], axis=0)
    q_flat = q_rows.reshape(rows * head_count, head_size)
    g_flat = grad_rows.reshape(rows * head_count, head_size)
    scores = jnp.dot(q_flat, all_keys.T, preferred_element_type=jnp.float32) * scale
    scores = scores.reshape(rows, head_count, 2 * rows)
    scores = jnp.where(allowed[:, None, :], scores, -1e30)
    top = jnp.max(scores, axis=2, keepdims=True)
    weights = jnp.exp(scores - top)
    prob = (weights / jnp.sum(weights, axis=2, keepdims=True)).reshape(rows * head_count, 2 * rows)
    prob_b = prob.astype(jnp.bfloat16)
    result = jnp.dot(prob_b, all_values, preferred_element_type=jnp.float32).astype(jnp.bfloat16)
    delta = jnp.sum(g_flat.astype(jnp.float32) * result.astype(jnp.float32), axis=1, keepdims=True)
    dprob = jnp.dot(g_flat, all_values.T, preferred_element_type=jnp.float32)
    dscore = (prob * (dprob - delta)).astype(jnp.bfloat16)
    dquery = (jnp.dot(dscore, all_keys, preferred_element_type=jnp.float32) * scale).astype(
        jnp.bfloat16
    )
    dkeys_all = jnp.dot(dscore.T, q_flat, preferred_element_type=jnp.float32) * scale
    dvalues_all = jnp.dot(prob_b.T, g_flat, preferred_element_type=jnp.float32)
    back_keys, back_values = (
        shifted(dkeys_all[rows:].astype(jnp.bfloat16), "ctx", -1).astype(jnp.float32),
        shifted(dvalues_all[rows:].astype(jnp.bfloat16), "ctx", -1).astype(jnp.float32),
    )
    dkeys = (dkeys_all[:rows] + back_keys).astype(jnp.bfloat16)
    dvalues = (dvalues_all[:rows] + back_values).astype(jnp.bfloat16)
    term = jnp.dot(x_rows.T, dvalues, preferred_element_type=jnp.float32)
    partial_sum = lax.psum_scatter(term, "dp", scatter_dimension=0, tiled=True)
    grad_w = lax.psum(partial_sum.astype(jnp.bfloat16), "ctx").astype(jnp.float32)
    attn_rows = result.reshape(rows, head_count * head_size)
    query_grads = dquery.reshape(rows, head_count * head_size)
    return (attn_rows[None], query_grads[None], dkeys[None], grad_w)


def solution(mesh):
    return jax.shard_map(
        shards,
        mesh=mesh,
        in_specs=(
            P("dp", "ctx", None),
            P(),
            P("dp", None),
            P("dp", "ctx", None),
            P("dp", "ctx", None),
            P("dp", "ctx", None),
        ),
        out_specs=(P("dp", "ctx", None), P("dp", "ctx", None), P("dp", "ctx", None), P("dp", None)),
        check_vma=False,
    )
```

profile of v0, /device:TPU:2, one launch (start us, length us, event | category | flops | bytes accessed | tf_op | source)
XLA Modules:
  0.0 833.3 jit_solution(6949532465269610790)
XLA Ops:
  8.0 15.3 %collective-permute-start = (bf16[128,128]{1,0:T(8,128)(2,1)}, bf16[128,128]{1,0:T(8,128)(2,1)S(1)}, u32[]{:S(2)}, u32[]{:S(2)}) collective-permute-start(bf16[128,128]{1,0:T(8,128)(2,1)} %bitcast.46), channel_id=1, source_target_pairs={{0,1},{1,2},{2,3},{3,4},{4,5},{5,6},{6,7},{7,0},{8,9},{9,10},{10,1... | collective-permute-start | bytes 98312 | tf_op jit(solution)/shard_map/ppermute | solution.py:12
  24.7 1.3 fusion.24
  26.0 1.3 fusion.21
  28.2 1.0 reshape_squeeze.7
  29.2 1.3 reshape_squeeze.6
  33.3 5.1 collective-permute-start.3
  38.4 7.6 collective-permute-done.3
  46.1 3.0 convolution_bitcast_fusion
  49.1 6.1 copy.19
  55.1 135.5 %all-gather.2.cloned.1.call-done = bf16[9216,128]{1,0:T(8,128)(2,1)} async-done(((bf16[96,128]{1,0:T(8,128)(2,1)}), bf16[9216,128]{1,0:T(8,128)(2,1)}) %all-gather.2.cloned.1.call-update) | async-done | bytes 2359312 | tf_op jit(solution)/shard_map/all_gather | solution.py:26
  190.7 2.4 fusion.11
  193.1 8.2 collective-permute-start.1
  201.3 2.0 copy.17
  203.4 3.1 collective-permute-done.1
  206.5 2.2 multiply_reduce_fusion
  208.7 1.7 fusion.4
  211.4 7.3 collective-permute-start.2
  219.2 1.0 broadcast_in_dim_reshape.7
  220.5 1.0 broadcast_in_dim_reshape.6
  221.6 2.6 collective-permute-done.2
  224.1 1.4 fusion.17
  225.5 540.4 %reduce-scatter.4.cloned.1.call-done = f32[96,128]{1,0:T(8,128)} async-done(((f32[9216,128]{1,0:T(8,128)}), f32[96,128]{1,0:T(8,128)}) %reduce-scatter.4.cloned.1.call-update) | async-done | bytes 49168
  766.0 0.9 copy.20
  766.9 58.9 %psum.7 = bf16[96,128]{0,1:T(8,128)(2,1)S(1)} all-reduce(bf16[96,128]{0,1:T(8,128)(2,1)S(1)} %copy.20), channel_id=1, replica_groups=mesh['dp'=96,'ctx'=8] {'ctx'}, use_global_device_ids=true, to_apply=%region_4.5 | all-reduce | flops 12288 | bytes 49152 | tf_op jit(solution)/shard_map/psum | solution.py:71
  (45 shorter events, 8.3 us)
Async XLA Ops:
  7.2 38.9 %copy-start = (bf16[1,128,9216]{2,1,0:T(8,128)(2,1)S(1)}, bf16[1,128,9216]{2,1,0:T(8,128)(2,1)}, u32[]{:S(2)}) copy-start(bf16[1,128,9216]{2,1,0:T(8,128)(2,1)} %param.6) | copy-start | bytes 7077892
  7.2 23.3 %copy-start.8 = (bf16[1,128,128]{2,1,0:T(8,128)(2,1)S(1)}, bf16[1,128,128]{2,1,0:T(8,128)(2,1)}, u32[]{:S(2)}) copy-start(bf16[1,128,128]{2,1,0:T(8,128)(2,1)} %param.10) | copy-start | bytes 98308
  7.2 21.0 %copy-start.7 = (bf16[1,128,2048]{2,1,0:T(8,128)(2,1)S(1)}, bf16[1,128,2048]{2,1,0:T(8,128)(2,1)}, u32[]{:S(2)}) copy-start(bf16[1,128,2048]{2,1,0:T(8,128)(2,1)} %param.11) | copy-start | bytes 1572868
  7.2 183.4 %all-gather.2.cloned.1.call-start = ((), (), s32[]{:S(2)}) async-start(), calls=%async_computation.1 | async-start | bytes 2383872 | tf_op jit(solution)/shard_map/all_gather | solution.py:26
  7.9 758.0 %reduce-scatter.4.cloned.1.call-start = ((), (), s32[]{:S(2)}) async-start(), calls=%async_computation.2 | async-start | bytes 4767744
  8.0 22.5 %collective-permute-start = (bf16[128,128]{1,0:T(8,128)(2,1)}, bf16[128,128]{1,0:T(8,128)(2,1)S(1)}, u32[]{:S(2)}, u32[]{:S(2)}) collective-permute-start(bf16[128,128]{1,0:T(8,128)(2,1)} %bitcast.46), channel_id=1, source_target_pairs={{0,1},{1,2},{2,3},{3,4},{4,5},{5,6},{6,7},{7,0},{8,9},{9,10},{10,1... | collective-permute-start | bytes 98312 | tf_op jit(solution)/shard_map/ppermute | solution.py:12
  30.5 0.8 copy-start.3
  30.5 1.1 copy-start.10
  31.1 1.4 copy-start.1
  31.6 1.2 copy-start.5
  33.3 12.8 %collective-permute-start.3 = (bf16[128,128]{1,0:T(8,128)(2,1)S(1)}, bf16[128,128]{1,0:T(8,128)(2,1)S(1)}, u32[]{:S(2)}, u32[]{:S(2)}) collective-permute-start(bf16[128,128]{1,0:T(8,128)(2,1)S(1)} %slice.39), channel_id=1, source_target_pairs={{0,7},{1,0},{2,1},{3,2},{4,3},{5,4},{6,5},{7,6},{8,15},{9,8},{10,9... | collective-permute-start | bytes 98312 | tf_op jit(solution)/shard_map/ppermute | solution.py:12
  193.1 13.4 %collective-permute-start.1 = (bf16[128,128]{1,0:T(8,128)(2,1)S(1)}, bf16[128,128]{1,0:T(8,128)(2,1)S(1)}, u32[]{:S(2)}, u32[]{:S(2)}) collective-permute-start(bf16[128,128]{1,0:T(8,128)(2,1)S(1)} %fusion.11), channel_id=1, source_target_pairs={{0,1},{1,2},{2,3},{3,4},{4,5},{5,6},{6,7},{7,0},{8,9},{9,10},{10,1... | collective-permute-start | bytes 98312 | tf_op jit(solution)/shard_map/ppermute | solution.py:12
  203.4 5.3 copy-start.2
  208.7 1.7 copy-start.4
  208.7 10.0 %copy-start.9 = (bf16[1,128,128]{2,1,0:T(8,128)(2,1)S(1)}, bf16[1,128,128]{2,1,0:T(8,128)(2,1)}, u32[]{:S(2)}) copy-start(bf16[1,128,128]{2,1,0:T(8,128)(2,1)} %param.10) | copy-start | bytes 98308
  208.7 10.0 %copy-start.11 = (bf16[128,128]{1,0:T(8,128)(2,1)S(1)}, bf16[128,128]{1,0:T(8,128)(2,1)}, u32[]{:S(2)}) copy-start(bf16[128,128]{1,0:T(8,128)(2,1)} %copy-done.10) | copy-start | bytes 98308
  210.4 9.9 %copy-start.6 = (bf16[2048,128]{0,1:T(8,128)(2,1)S(1)}, bf16[2048,128]{0,1:T(8,128)(2,1)}, u32[]{:S(2)}) copy-start(bf16[2048,128]{0,1:T(8,128)(2,1)} %get-tuple-element.25) | copy-start | bytes 1572868
  211.4 12.7 %collective-permute-start.2 = (bf16[128,128]{1,0:T(8,128)(2,1)}, bf16[128,128]{1,0:T(8,128)(2,1)}, u32[]{:S(2)}, u32[]{:S(2)}) collective-permute-start(bf16[128,128]{1,0:T(8,128)(2,1)} %slice.40), channel_id=1, source_target_pairs={{0,7},{1,0},{2,1},{3,2},{4,3},{5,4},{6,5},{7,6},{8,15},{9,8},{10,9... | collective-permute-start | bytes 98312 | tf_op jit(solution)/shard_map/ppermute | solution.py:12
Sparse Core Ops, SparseCore 0:
  10.5 180.0 all-gather.1
  193.8 572.1 reduce-scatter.3
where the time goes:
time: 834 us; the launch traced here: 833 us
  waiting for transfers between devices  690 us (83%)
  blocking collectives  58.9 us (7%)
  starting transfers between devices  36 us (4%)
  local copies, waits for them, and re-layouts  18.3 us (2%)
  between operations  14.3 us (2%)
  matrix products  11.1 us (1%)
    unnamed x3, waiting for transfers between devices  541 us
    all_gather x1, waiting for transfers between devices, shards(): lax.all_gather(w_value, 'dp', axis=0, tiled=True)  136 us
    psum x1, blocking collectives, shards(): lax.psum(partial_sum.astype(jnp.bfloat16), 'ctx').astype(jnp.float32)  58.9 us
    ppermute x4, starting transfers between devices, shifted(): return lax.ppermute(value, axis, pairs)  35.9 us
  transfers between devices with their start and end apart: 6, of which 5 were waited for; matrix products, arithmetic and copies ran while one was open for 4% of the time, Pallas kernels for 0%

commit v1 on v0

v1 whole, which is shorter than its diff:
```python
import jax
import jax.numpy as jnp
from jax import lax
from jax.sharding import Mesh
from jax.sharding import PartitionSpec as P

BLK = 64
NY, NZ, NC, NX, NH = 8, 6, 2, 4, 2
DP = ("y", "zl", "c")
CTX = ("x", "zh")
BF = jnp.bfloat16
F32 = jnp.float32


def shifted(value, axis, steps):
    count = lax.axis_size(axis)
    pairs = [(source, (source + steps) % count) for source in range(count)]
    return lax.ppermute(value, axis, pairs)


def exchanged(value, axis):
    return lax.all_to_all(value, axis, 0, 0, tiled=True)


def gathered_weight(w):
    part = w.shape[0] // NX
    xi = lax.axis_index("x")
    piece = lax.dynamic_slice_in_dim(w, part * xi, part, 0)
    own = exchanged(jnp.broadcast_to(piece[None], (NY * NZ,) + piece.shape), ("y", "zl"))
    left = shifted(own, "x", 1)
    right = shifted(own, "x", -1)
    half = NY * NZ // 2
    far = jnp.concatenate([shifted(left[:half], "x", 1), shifted(right[half:], "x", -1)], axis=0)
    turn = jnp.stack([own, right, far, left, own, right, far], axis=0)
    mine = lax.dynamic_slice_in_dim(turn, (NX - xi) % NX, NX, 0)
    theirs = shifted(mine, "c", 1)
    first = lax.axis_index("c") == 0
    both = jnp.stack([jnp.where(first, mine, theirs), jnp.where(first, theirs, mine)], axis=0)
    return both.transpose(2, 0, 1, 3, 4).reshape(NY * NZ * NC * NX * part, w.shape[1])


def scattered_sum(term):
    part = term.shape[0] // (NY * NZ * NC * NX)
    hd = term.shape[1]
    blocks = term.reshape(NY * NZ, NC, NX, part, hd)
    ci = lax.axis_index("c")
    mine = lax.dynamic_index_in_dim(blocks, ci, 1, keepdims=False)
    theirs = lax.dynamic_index_in_dim(blocks, 1 - ci, 1, keepdims=False).astype(BF)
    total = mine + shifted(theirs, "c", 1).astype(F32)
    sent = total.astype(BF).transpose(1, 0, 2, 3)
    total = jnp.sum(exchanged(sent, "x").astype(F32), axis=0)
    sent = total.astype(BF).reshape(NY, NZ, part, hd)
    total = jnp.sum(exchanged(sent, "y").astype(F32), axis=0)
    sent = total.astype(BF)[:, None]
    sent = jnp.broadcast_to(sent, (NZ, NH, part, hd)).reshape(NZ * NH, part, hd)
    total = jnp.sum(exchanged(sent, ("zl", "zh")).astype(F32), axis=0)
    sent = jnp.broadcast_to(total.astype(BF)[None], (NX, part, hd))
    return exchanged(sent, "x").reshape(NX * part, hd).astype(F32)


def shards(inputs, block_order, w_value, query, keys, out_grad):
    x_rows = inputs[0]
    q_rows = query[0]
    k_rows = keys[0]
    grad_rows = out_grad[0]
    rows = x_rows.shape[0]
    head_size = k_rows.shape[1]
    head_count = q_rows.shape[1] // head_size
    scale = 1.0 / head_size**0.5
    far_keys = shifted(k_rows, CTX, 1)
    w_full = gathered_weight(w_value)

    index = lax.axis_index(CTX)
    count = lax.axis_size(CTX)
    before = (index + count - 1) % count
    local_iota = jnp.arange(rows, dtype=jnp.int32)

    def places(owner):
        slots = lax.dynamic_slice_in_dim(block_order, 2 * owner, 2, 0)
        return slots[local_iota // BLK] * BLK + local_iota % BLK

    mine = places(index)
    theirs = places(before)
    key_place = jnp.concatenate([mine, theirs], axis=0)
    allowed = key_place[None, :] <= mine[:, None]
    all_keys = jnp.concatenate([k_rows, far_keys], axis=0)
    q_flat = q_rows.reshape(rows * head_count, head_size)
    g_flat = grad_rows.reshape(rows * head_count, head_size)
    scores = jnp.dot(q_flat, all_keys.T, preferred_element_type=F32) * scale
    scores = scores.reshape(rows, head_count, 2 * rows)
    scores = jnp.where(allowed[:, None, :], scores, -1e30)
    top = jnp.max(scores, axis=2, keepdims=True)
    weights = jnp.exp(scores - top)
    prob = (weights / jnp.sum(weights, axis=2, keepdims=True)).reshape(rows * head_count, 2 * rows)
    prob_b = prob.astype(BF)
    dvalues_all = jnp.dot(prob_b.T, g_flat, preferred_element_type=F32)
    back_values = shifted(dvalues_all[rows:].astype(BF), CTX, -1).astype(F32)
    dvalues = (dvalues_all[:rows] + back_values).astype(BF)
    term = jnp.dot(x_rows.T, dvalues, preferred_element_type=F32)
    grad_w = scattered_sum(term)

    values = jnp.dot(x_rows, w_full, preferred_element_type=F32).astype(BF)
    far_values = shifted(values, CTX, 1)
    all_values = jnp.concatenate([values, far_values], axis=0)
    result = jnp.dot(prob_b, all_values, preferred_element_type=F32).astype(BF)
    delta = jnp.sum(g_flat.astype(F32) * result.astype(F32), axis=1, keepdims=True)
    dprob = jnp.dot(g_flat, all_values.T, preferred_element_type=F32)
    dscore = (prob * (dprob - delta)).astype(BF)
    dquery = (jnp.dot(dscore, all_keys, preferred_element_type=F32) * scale).astype(BF)
    dkeys_all = jnp.dot(dscore.T, q_flat, preferred_element_type=F32) * scale
    back_keys = shifted(dkeys_all[rows:].astype(BF), CTX, -1).astype(F32)
    dkeys = (dkeys_all[:rows] + back_keys).astype(BF)
    attn_rows = result.reshape(rows, head_count * head_size)
    query_grads = dquery.reshape(rows, head_count * head_size)
    return (attn_rows[None], query_grads[None], dkeys[None], grad_w)


def solution(mesh):
    fine = Mesh(mesh.devices.reshape(NY, NZ, NC, NX, NH), ("y", "zl", "c", "x", "zh"))
    return jax.shard_map(
        shards,
        mesh=fine,
        in_specs=(
            P(DP, CTX, None),
            P(),
            P(DP, None),
            P(DP, CTX, None),
            P(DP, CTX, None),
            P(DP, CTX, None),
        ),
        out_specs=(P(DP, CTX, None), P(DP, CTX, None), P(DP, CTX, None), P(DP, None)),
        check_vma=False,
    )
```

time: 834 us -> 177 us (0.21)
  waiting for transfers between devices: 690 us -> 30.8 us
  blocking collectives: 58.9 us -> 0 us
  starting transfers between devices: 36 us -> 84.5 us
  local copies, waits for them, and re-layouts: 18.3 us -> 32.3 us
  between operations: 14.3 us -> 1.06 us
  other arithmetic: 4.72 us -> 14.6 us
    unnamed x3 -> x0, waiting for transfers between devices: 541 us -> none
    all_gather x1 -> x0, waiting for transfers between devices: 136 us -> none  [shards(): lax.all_gather(w_value, 'dp', axis=0, tiled=True)]
    psum x1 -> x0, blocking collectives: 58.9 us -> none  [shards(): lax.psum(partial_sum.astype(jnp.bfloat16), 'ctx').astype(jnp.float32)]
    all_to_all x0 -> x5, starting transfers between devices: none -> 38.9 us  [exchanged(): return lax.all_to_all(value, axis, 0, 0, tiled=True)]
    all_to_all x0 -> x5, waiting for transfers between devices: none -> 15.6 us  [exchanged(): return lax.all_to_all(value, axis, 0, 0, tiled=True)]
    ppermute x4 -> x10, starting transfers between devices: 35.9 us -> 45.6 us  [shifted(): return lax.ppermute(value, axis, pairs)]
  transfers between devices with their start and end apart: 6 -> 15, of which waited for: 5 -> 7; matrix products, arithmetic and copies ran while one was open for 4% -> 32% of each run, Pallas kernels for 0% -> 0%
where the time goes in v1:
time: 177 us; the launch traced here: 175 us
  starting transfers between devices  84.5 us (48%)
  local copies, waits for them, and re-layouts  32.3 us (18%)
  waiting for transfers between devices  30.8 us (17%)
  other arithmetic  14.6 us (8%)
  matrix products  11.9 us (7%)
    ppermute x10, starting transfers between devices, shifted(): return lax.ppermute(value, axis, pairs)  45.6 us
    all_to_all x5, starting transfers between devices, exchanged(): return lax.all_to_all(value, axis, 0, 0, tiled=True)  38.9 us
    all_to_all x5, waiting for transfers between devices, exchanged(): return lax.all_to_all(value, axis, 0, 0, tiled=True)  15.6 us
    ppermute x10, waiting for transfers between devices, shifted(): return lax.ppermute(value, axis, pairs)  15.2 us
    dot_general x1, local copies, waits for them, and re-layouts, shards(): term = jnp.dot(x_rows.T, dvalues, preferred_element_type=F32)  6.04 us
    unnamed x25, local copies, waits for them, and re-layouts  4.72 us
    another operation x2, local copies, waits for them, and re-layouts, shards(): g_flat = grad_rows.reshape(rows * head_count, head_size)  4.12 us
    dot_general x1, matrix products, shards(): term = jnp.dot(x_rows.T, dvalues, preferred_element_type=F32)  3.68 us
  transfers between devices with their start and end apart: 15, of which 7 were waited for; matrix products, arithmetic and copies ran while one was open for 32% of the time, Pallas kernels for 0%

profile of v1, /device:TPU:2, one launch (start us, length us, event | category | flops | bytes accessed | tf_op | source)
XLA Modules:
  0.0 175.2 jit_solution(7411407403501268557)
XLA Ops:
  0.6 15.3 %collective-permute-start = (bf16[128,128]{1,0:T(8,128)(2,1)}, bf16[128,128]{1,0:T(8,128)(2,1)S(1)}, u32[]{:S(2)}, u32[]{:S(2)}) collective-permute-start(bf16[128,128]{1,0:T(8,128)(2,1)} %bitcast.101), channel_id=1, source_target_pairs={{0,1},{1,2},{2,3},{3,4},{4,5},{5,6},{6,7},{7,0},{8,9},{9,10},{10,1... | collective-permute-start | bytes 98312 | tf_op jit(solution)/shard_map/ppermute | solution.py:18
  17.4 12.7 %all-to-all-start = ((bf16[48,24,128]{2,1,0:T(8,128)(2,1)}), bf16[48,24,128]{2,1,0:T(8,128)(2,1)}, u32[]{:S(2)}, u32[]{:S(2)}) async-start(bf16[48,24,128]{2,1,0:T(8,128)(2,1)} %broadcast_in_dim.25), calls=%async_computation | async-start | bytes 589824 | tf_op jit(solution)/shard_map/all_to_all | solution.py:22
  32.1 2.6 %fusion.29 = (s32[128]{0:T(128)S(1)}, s32[128]{0:T(128)S(1)}) fusion(s32[]{:T(128)} %bitcast.4, s32[]{:T(128)} %bitcast.3, s32[]{:T(128)} %bitcast.1, s32[]{:T(128)} %bitcast), kind=kLoop, calls=%fused_computation.62 | loop fusion | flops 3072 | bytes 1040 | tf_op jit(solution)/shard_map/add | solution.py:80
  42.3 4.2 %collective-permute-start.8 = (bf16[128,128]{1,0:T(8,128)(2,1)}, bf16[128,128]{1,0:T(8,128)(2,1)}, u32[]{:S(2)}, u32[]{:S(2)}) collective-permute-start(bf16[128,128]{1,0:T(8,128)(2,1)} %slice.49), channel_id=1, source_target_pairs={{0,7},{1,0},{2,1},{3,2},{4,3},{5,4},{6,5},{7,6},{8,15},{9,8},{10,9... | collective-permute-start | bytes 98312 | tf_op jit(solution)/shard_map/ppermute | solution.py:18
  46.6 8.6 %collective-permute-done.8 = bf16[128,128]{1,0:T(8,128)(2,1)} collective-permute-done((bf16[128,128]{1,0:T(8,128)(2,1)}, bf16[128,128]{1,0:T(8,128)(2,1)}, u32[]{:S(2)}, u32[]{:S(2)}) %collective-permute-start.8) | collective-permute-done | bytes 32800 | tf_op jit(solution)/shard_map/ppermute | solution.py:18
  55.1 3.7 %convolution_bitcast_fusion = f32[9216,128]{0,1:T(8,128)} fusion(bf16[1,128,9216]{2,1,0:T(8,128)(2,1)S(1)} %copy-done, f32[256,128]{1,0:T(8,128)S(1)} %fusion.41, bf16[128,128]{1,0:T(8,128)(2,1)} %collective-permute-done.8), kind=kOutput, calls=%fused_computation | convolution fusion | flops 302039040 | bytes 7176192 | tf_op jit(solution)/shard_map/dot_general | solution.py:99
  58.8 6.0 %copy.40 = f32[9216,128]{1,0:T(8,128)} copy(f32[9216,128]{0,1:T(8,128)} %convolution_bitcast_fusion) | data formatting | bytes 9437184 | tf_op jit(solution)/shard_map/dot_general | solution.py:99
  67.0 3.7 %collective-permute-start.2 = (bf16[48,24,128]{2,1,0:T(8,128)(2,1)}, bf16[48,24,128]{2,1,0:T(8,128)(2,1)S(1)}, u32[]{:S(2)}, u32[]{:S(2)}) collective-permute-start(bf16[48,24,128]{2,1,0:T(8,128)(2,1)} %all-to-all-done), channel_id=1, source_target_pairs={{0,2},{2,4},{4,6},{6,0},{1,3},{3,5},{5,7},{7,1},{8,10},{10,12},{12... | collective-permute-start | bytes 884744 | tf_op jit(solution)/shard_map/ppermute | solution.py:18
  70.7 2.9 %fusion.12 = bf16[48,4,24,128]{3,2,1,0:T(8,128)(2,1)} fusion(f32[48,2,4,24,128]{4,3,2,1,0:T(8,128)} %bitcast.95, s32[]{:T(128)S(6)} %select_n.105), kind=kLoop, calls=%fused_computation.21 | loop fusion | bytes 2359300 | tf_op jit(solution)/shard_map/convert_element_type | solution.py:48
  76.5 3.2 %collective-permute-start.4 = (bf16[24,24,128]{2,1,0:T(8,128)(2,1)S(1)}, bf16[24,24,128]{2,1,0:T(8,128)(2,1)S(1)}, u32[]{:S(2)}, u32[]{:S(2)}) collective-permute-start(bf16[24,24,128]{2,1,0:T(8,128)(2,1)S(1)} %slice.33), channel_id=1, source_target_pairs={{0,6},{2,0},{4,2},{6,4},{1,7},{3,1},{5,3},{7,5},{8,14},{10,8},{12,... | collective-permute-start | bytes 442376 | tf_op jit(solution)/shard_map/ppermute | solution.py:18
  79.8 2.7 %collective-permute-start.3 = (bf16[24,24,128]{2,1,0:T(8,128)(2,1)S(1)}, bf16[24,24,128]{2,1,0:T(8,128)(2,1)S(1)}, u32[]{:S(2)}, u32[]{:S(2)}) collective-permute-start(bf16[24,24,128]{2,1,0:T(8,128)(2,1)S(1)} %slice.32), channel_id=1, source_target_pairs={{0,2},{2,4},{4,6},{6,0},{1,3},{3,5},{5,7},{7,1},{8,10},{10,12},{12... | collective-permute-start | bytes 442376 | tf_op jit(solution)/shard_map/ppermute | solution.py:18
  84.7 4.4 %collective-permute-done.3 = bf16[24,24,128]{2,1,0:T(8,128)(2,1)S(1)} collective-permute-done((bf16[24,24,128]{2,1,0:T(8,128)(2,1)S(1)}, bf16[24,24,128]{2,1,0:T(8,128)(2,1)S(1)}, u32[]{:S(2)}, u32[]{:S(2)}) %collective-permute-start.3) | collective-permute-done | bytes 147488 | tf_op jit(solution)/shard_map/ppermute | solution.py:18
  94.9 2.4 %fusion.13 = bf16[4,48,24,128]{3,2,0,1:T(8,128)(2,1)S(1)} fusion(bf16[48,4,24,128]{3,2,1,0:T(8,128)(2,1)} %collective-permute-done.9, f32[48,2,4,24,128]{4,3,2,1,0:T(8,128)} %bitcast.96, s32[]{:T(128)S(6)} %select_n.104), kind=kLoop, calls=%fused_computation.22 | loop fusion | flops 1769472 | bytes 4718596 | tf_op jit(solution)/shard_map/transpose | solution.py:50
  98.5 7.2 %all-to-all-start.1 = ((bf16[4,48,24,128]{3,2,1,0:T(8,128)(2,1)}), bf16[4,48,24,128]{3,2,1,0:T(8,128)(2,1)}, u32[]{:S(2)}, u32[]{:S(2)}) async-start(bf16[4,48,24,128]{3,2,1,0:T(8,128)(2,1)} %copy.41), calls=%async_computation.1 | async-start | bytes 2359296 | tf_op jit(solution)/shard_map/all_to_all | solution.py:22
  108.5 5.0 %collective-permute-start.6 = (bf16[128,128]{1,0:T(8,128)(2,1)S(1)}, bf16[128,128]{1,0:T(8,128)(2,1)S(1)}, u32[]{:S(2)}, u32[]{:S(2)}) collective-permute-start(bf16[128,128]{1,0:T(8,128)(2,1)S(1)} %fusion.17), channel_id=1, source_target_pairs={{0,1},{1,2},{2,3},{3,4},{4,5},{5,6},{6,7},{7,0},{8,9},{9,10},{10,1... | collective-permute-start | bytes 98312 | tf_op jit(solution)/shard_map/ppermute | solution.py:18
  115.6 6.2 %all-to-all-done.1 = bf16[4,48,24,128]{3,2,1,0:T(8,128)(2,1)} async-done(((bf16[4,48,24,128]{3,2,1,0:T(8,128)(2,1)}), bf16[4,48,24,128]{3,2,1,0:T(8,128)(2,1)}, u32[]{:S(2)}, u32[]{:S(2)}) %all-to-all-start.1) | async-done | bytes 1179680 | tf_op jit(solution)/shard_map/all_to_all | solution.py:22
  121.8 2.2 %reduce_sum.56 = bf16[48,24,128]{2,1,0:T(8,128)(2,1)} reduce(bf16[4,48,24,128]{3,2,1,0:T(8,128)(2,1)} %all-to-all-done.1, bf16[]{:T(256)} %constant.108.clone.1), dimensions={0}, to_apply=%region_3.4 | reduce | flops 442368 | bytes 1474562 | tf_op jit(solution)/shard_map/reduce_sum | solution.py:51
  124.0 7.1 %all-to-all-start.2 = ((bf16[8,6,24,128]{3,2,1,0:T(8,128)(2,1)}), bf16[8,6,24,128]{3,2,1,0:T(8,128)(2,1)}, u32[]{:S(2)}, u32[]{:S(2)}) async-start(bf16[8,6,24,128]{3,2,1,0:T(8,128)(2,1)} %bitcast.99), calls=%async_computation.2 | async-start | bytes 589824 | tf_op jit(solution)/shard_map/all_to_all | solution.py:22
  131.2 2.3 %multiply_reduce_fusion = (f32[2048]{0:T(1024)S(1)}, bf16[2048,128]{0,1:T(8,128)(2,1)}) fusion(bf16[2048,128]{0,1:T(8,128)(2,1)} %copy.39, bf16[2048,256]{0,1:T(8,128)(2,1)S(1)} %fusion.20, bf16[128,128]{1,0:T(8,128)(2,1)S(1)} %collective-permute-done.6, bf16[128,128]{1,0:T(8,128)(2,1)S(1)} %fusion.17), kind=kOutput, calls=%fused_computation.28 | convolution fusion | flops 135657472 | bytes 2170880 | tf_op jit(solution)/shard_map/dot_general | solution.py:105
  136.3 5.6 %collective-permute-start.7 = (bf16[128,128]{1,0:T(8,128)(2,1)}, bf16[128,128]{1,0:T(8,128)(2,1)}, u32[]{:S(2)}, u32[]{:S(2)}) collective-permute-start(bf16[128,128]{1,0:T(8,128)(2,1)} %slice.50), channel_id=1, source_target_pairs={{0,7},{1,0},{2,1},{3,2},{4,3},{5,4},{6,5},{7,6},{8,15},{9,8},{10,9... | collective-permute-start | bytes 98312 | tf_op jit(solution)/shard_map/ppermute | solution.py:18
  146.7 7.0 %all-to-all-start.3 = ((bf16[12,24,128]{2,1,0:T(8,128)(2,1)}), bf16[12,24,128]{2,1,0:T(8,128)(2,1)}, u32[]{:S(2)}, u32[]{:S(2)}) async-start(bf16[12,24,128]{2,1,0:T(8,128)(2,1)} %bitcast.100), calls=%async_computation.3 | async-start | bytes 147456 | tf_op jit(solution)/shard_map/all_to_all | solution.py:22
  159.1 5.0 %all-to-all-done.3 = bf16[12,24,128]{2,1,0:T(8,128)(2,1)} async-done(((bf16[12,24,128]{2,1,0:T(8,128)(2,1)}), bf16[12,24,128]{2,1,0:T(8,128)(2,1)}, u32[]{:S(2)}, u32[]{:S(2)}) %all-to-all-start.3) | async-done | bytes 73760 | tf_op jit(solution)/shard_map/all_to_all | solution.py:22
  165.7 4.9 %all-to-all-start.4 = ((bf16[4,24,128]{2,1,0:T(8,128)(2,1)}), bf16[4,24,128]{2,1,0:T(8,128)(2,1)S(1)}, u32[]{:S(2)}, u32[]{:S(2)}) async-start(bf16[4,24,128]{2,1,0:T(8,128)(2,1)} %broadcast_in_dim.28), calls=%async_computation.4 | async-start | bytes 49152 | tf_op jit(solution)/shard_map/all_to_all | solution.py:22
  172.0 2.6 %all-to-all-done.4 = bf16[4,24,128]{2,1,0:T(8,128)(2,1)S(1)} async-done(((bf16[4,24,128]{2,1,0:T(8,128)(2,1)}), bf16[4,24,128]{2,1,0:T(8,128)(2,1)S(1)}, u32[]{:S(2)}, u32[]{:S(2)}) %all-to-all-start.4) | async-done | bytes 24608 | tf_op jit(solution)/shard_map/all_to_all | solution.py:22
  (77 shorter events, 46.6 us)
Async XLA Ops:
  0.6 54.5 %copy-start = (bf16[1,128,9216]{2,1,0:T(8,128)(2,1)S(1)}, bf16[1,128,9216]{2,1,0:T(8,128)(2,1)}, u32[]{:S(2)}) copy-start(bf16[1,128,9216]{2,1,0:T(8,128)(2,1)} %param.6) | copy-start | bytes 7077892
  0.6 38.3 %collective-permute-start = (bf16[128,128]{1,0:T(8,128)(2,1)}, bf16[128,128]{1,0:T(8,128)(2,1)S(1)}, u32[]{:S(2)}, u32[]{:S(2)}) collective-permute-start(bf16[128,128]{1,0:T(8,128)(2,1)} %bitcast.101), channel_id=1, source_target_pairs={{0,1},{1,2},{2,3},{3,4},{4,5},{5,6},{6,7},{7,0},{8,9},{9,10},{10,1... | collective-permute-start | bytes 98312 | tf_op jit(solution)/shard_map/ppermute | solution.py:18
  17.4 21.6 %copy-start.8 = (bf16[1,128,128]{2,1,0:T(8,128)(2,1)S(1)}, bf16[1,128,128]{2,1,0:T(8,128)(2,1)}, u32[]{:S(2)}) copy-start(bf16[1,128,128]{2,1,0:T(8,128)(2,1)} %param.10) | copy-start | bytes 98308
  17.4 47.5 %all-to-all-start = ((bf16[48,24,128]{2,1,0:T(8,128)(2,1)}), bf16[48,24,128]{2,1,0:T(8,128)(2,1)}, u32[]{:S(2)}, u32[]{:S(2)}) async-start(bf16[48,24,128]{2,1,0:T(8,128)(2,1)} %broadcast_in_dim.25), calls=%async_computation | async-start | bytes 589824 | tf_op jit(solution)/shard_map/all_to_all | solution.py:22
  39.0 1.1 copy-start.9
  39.5 1.3 copy-start.1
  40.1 1.2 copy-start.5
  42.3 12.8 %collective-permute-start.8 = (bf16[128,128]{1,0:T(8,128)(2,1)}, bf16[128,128]{1,0:T(8,128)(2,1)}, u32[]{:S(2)}, u32[]{:S(2)}) collective-permute-start(bf16[128,128]{1,0:T(8,128)(2,1)} %slice.49), channel_id=1, source_target_pairs={{0,7},{1,0},{2,1},{3,2},{4,3},{5,4},{6,5},{7,6},{8,15},{9,8},{10,9... | collective-permute-start | bytes 98312 | tf_op jit(solution)/shard_map/ppermute | solution.py:18
  64.9 11.6 %collective-permute-start.1 = (bf16[48,24,128]{2,1,0:T(8,128)(2,1)}, bf16[48,24,128]{2,1,0:T(8,128)(2,1)S(1)}, u32[]{:S(2)}, u32[]{:S(2)}) collective-permute-start(bf16[48,24,128]{2,1,0:T(8,128)(2,1)} %all-to-all-done), channel_id=1, source_target_pairs={{0,6},{2,0},{4,2},{6,4},{1,7},{3,1},{5,3},{7,5},{8,14},{10,8},{12,... | collective-permute-start | bytes 884744 | tf_op jit(solution)/shard_map/ppermute | solution.py:18
  67.0 12.8 %collective-permute-start.2 = (bf16[48,24,128]{2,1,0:T(8,128)(2,1)}, bf16[48,24,128]{2,1,0:T(8,128)(2,1)S(1)}, u32[]{:S(2)}, u32[]{:S(2)}) collective-permute-start(bf16[48,24,128]{2,1,0:T(8,128)(2,1)} %all-to-all-done), channel_id=1, source_target_pairs={{0,2},{2,4},{4,6},{6,0},{1,3},{3,5},{5,7},{7,1},{8,10},{10,12},{12... | collective-permute-start | bytes 884744 | tf_op jit(solution)/shard_map/ppermute | solution.py:18
  73.6 21.3 %collective-permute-start.9 = (bf16[48,4,24,128]{3,2,1,0:T(8,128)(2,1)}, bf16[48,4,24,128]{3,2,1,0:T(8,128)(2,1)}, u32[]{:S(2)}, u32[]{:S(2)}) collective-permute-start(bf16[48,4,24,128]{3,2,1,0:T(8,128)(2,1)} %fusion.12), channel_id=1, source_target_pairs={{0,8},{8,0},{1,9},{9,1},{2,10},{10,2},{3,11},{11,3},{4,12},{12,4},... | collective-permute-start | bytes 3538952 | tf_op jit(solution)/shard_map/ppermute | solution.py:18
  76.5 8.1 %collective-permute-start.4 = (bf16[24,24,128]{2,1,0:T(8,128)(2,1)S(1)}, bf16[24,24,128]{2,1,0:T(8,128)(2,1)S(1)}, u32[]{:S(2)}, u32[]{:S(2)}) collective-permute-start(bf16[24,24,128]{2,1,0:T(8,128)(2,1)S(1)} %slice.33), channel_id=1, source_target_pairs={{0,6},{2,0},{4,2},{6,4},{1,7},{3,1},{5,3},{7,5},{8,14},{10,8},{12,... | collective-permute-start | bytes 442376 | tf_op jit(solution)/shard_map/ppermute | solution.py:18
  79.8 9.4 %collective-permute-start.3 = (bf16[24,24,128]{2,1,0:T(8,128)(2,1)S(1)}, bf16[24,24,128]{2,1,0:T(8,128)(2,1)S(1)}, u32[]{:S(2)}, u32[]{:S(2)}) collective-permute-start(bf16[24,24,128]{2,1,0:T(8,128)(2,1)S(1)} %slice.32), channel_id=1, source_target_pairs={{0,2},{2,4},{4,6},{6,0},{1,3},{3,5},{5,7},{7,1},{8,10},{10,12},{12... | collective-permute-start | bytes 442376 | tf_op jit(solution)/shard_map/ppermute | solution.py:18
  90.4 1.4 copy-start.6
  93.0 12.7 %collective-permute-start.5 = (bf16[4,48,24,128]{3,2,0,1:T(8,128)(2,1)}, bf16[4,48,24,128]{3,2,0,1:T(8,128)(2,1)}, u32[]{:S(2)}, u32[]{:S(2)}) collective-permute-start(bf16[4,48,24,128]{3,2,0,1:T(8,128)(2,1)} %constant_dynamic-slice_fusion), channel_id=1, source_target_pairs={{0,8},{8,0},{1,9},{9,1},{2,10},{10,2},{3,11},{11,3},{4,12},{12,4},... | collective-permute-start | bytes 3538952 | tf_op jit(solution)/shard_map/ppermute | solution.py:18
  98.5 23.3 %all-to-all-start.1 = ((bf16[4,48,24,128]{3,2,1,0:T(8,128)(2,1)}), bf16[4,48,24,128]{3,2,1,0:T(8,128)(2,1)}, u32[]{:S(2)}, u32[]{:S(2)}) async-start(bf16[4,48,24,128]{3,2,1,0:T(8,128)(2,1)} %copy.41), calls=%async_computation.1 | async-start | bytes 2359296 | tf_op jit(solution)/shard_map/all_to_all | solution.py:22
  108.5 22.6 %collective-permute-start.6 = (bf16[128,128]{1,0:T(8,128)(2,1)S(1)}, bf16[128,128]{1,0:T(8,128)(2,1)S(1)}, u32[]{:S(2)}, u32[]{:S(2)}) collective-permute-start(bf16[128,128]{1,0:T(8,128)(2,1)S(1)} %fusion.17), channel_id=1, source_target_pairs={{0,1},{1,2},{2,3},{3,4},{4,5},{5,6},{6,7},{7,0},{8,9},{9,10},{10,1... | collective-permute-start | bytes 98312 | tf_op jit(solution)/shard_map/ppermute | solution.py:18
  124.0 19.6 %all-to-all-start.2 = ((bf16[8,6,24,128]{3,2,1,0:T(8,128)(2,1)}), bf16[8,6,24,128]{3,2,1,0:T(8,128)(2,1)}, u32[]{:S(2)}, u32[]{:S(2)}) async-start(bf16[8,6,24,128]{3,2,1,0:T(8,128)(2,1)} %bitcast.99), calls=%async_computation.2 | async-start | bytes 589824 | tf_op jit(solution)/shard_map/all_to_all | solution.py:22
  131.2 2.4 %copy-start.2 = (f32[2048,256]{0,1:T(8,128)S(1)}, f32[2048,256]{0,1:T(8,128)}, u32[]{:S(2)}) copy-start(f32[2048,256]{0,1:T(8,128)} %copy-done.1) | copy-start | bytes 6291460
  133.5 1.7 copy-start.4
  136.3 34.4 %collective-permute-start.7 = (bf16[128,128]{1,0:T(8,128)(2,1)}, bf16[128,128]{1,0:T(8,128)(2,1)}, u32[]{:S(2)}, u32[]{:S(2)}) collective-permute-start(bf16[128,128]{1,0:T(8,128)(2,1)} %slice.50), channel_id=1, source_target_pairs={{0,7},{1,0},{2,1},{3,2},{4,3},{5,4},{6,5},{7,6},{8,15},{9,8},{10,9... | collective-permute-start | bytes 98312 | tf_op jit(solution)/shard_map/ppermute | solution.py:18
  146.7 17.5 %all-to-all-start.3 = ((bf16[12,24,128]{2,1,0:T(8,128)(2,1)}), bf16[12,24,128]{2,1,0:T(8,128)(2,1)}, u32[]{:S(2)}, u32[]{:S(2)}) async-start(bf16[12,24,128]{2,1,0:T(8,128)(2,1)} %bitcast.100), calls=%async_computation.3 | async-start | bytes 147456 | tf_op jit(solution)/shard_map/all_to_all | solution.py:22
  155.7 2.4 %copy-start.7 = (bf16[2048,128]{1,0:T(8,128)(2,1)S(1)}, bf16[2048,128]{1,0:T(8,128)(2,1)}, u32[]{:S(2)}) copy-start(bf16[2048,128]{1,0:T(8,128)(2,1)} %fusion.5) | copy-start | bytes 1572868
  165.7 8.9 %all-to-all-start.4 = ((bf16[4,24,128]{2,1,0:T(8,128)(2,1)}), bf16[4,24,128]{2,1,0:T(8,128)(2,1)S(1)}, u32[]{:S(2)}, u32[]{:S(2)}) async-start(bf16[4,24,128]{2,1,0:T(8,128)(2,1)} %broadcast_in_dim.28), calls=%async_computation.4 | async-start | bytes 49152 | tf_op jit(solution)/shard_map/all_to_all | solution.py:22
  (1 other events, 0.8 us)

commit v2 on v1

v2 whole, which is shorter than its diff:
```python
import functools

import jax
import jax.numpy as jnp
from jax import lax
from jax.experimental import pallas as pl
from jax.experimental.pallas import tpu as pltpu
from jax.sharding import Mesh
from jax.sharding import PartitionSpec as P

BLK = 64
NY, NZ, NC, NX, NH = 8, 6, 2, 4, 2
DP = ("y", "zl", "c")
CTX = ("x", "zh")
BF = jnp.bfloat16
F32 = jnp.float32
VM = pl.BlockSpec(memory_space=pltpu.VMEM)
SM = pl.BlockSpec(memory_space=pltpu.SMEM)


def in_hbm(value):
    return pltpu.with_memory_space_constraint(value, pltpu.HBM)


def shifted(value, axis, steps):
    count = lax.axis_size(axis)
    pairs = [(source, (source + steps) % count) for source in range(count)]
    return lax.ppermute(value, axis, pairs)


def exchanged(value, axis):
    return lax.all_to_all(value, axis, 0, 0, tiled=True)


def kernel(body, ins, outs, flops, limit=24 * 2**20):
    size = sum(o.size * o.dtype.itemsize for o in outs)
    return pl.pallas_call(
        body,
        out_shape=outs,
        in_specs=ins,
        out_specs=[VM] * len(outs),
        cost_estimate=pl.CostEstimate(flops=flops, bytes_accessed=2 * size, transcendentals=0),
        compiler_params=pltpu.CompilerParams(vmem_limit_bytes=limit),
    )


def dot(a, b, ca, cb):
    return lax.dot_general(a, b, (((ca,), (cb,)), ((), ())), preferred_element_type=F32)


def places(order, owner, shape, axis):
    at = lax.broadcasted_iota(jnp.int32, shape, axis)
    low, high = order[2 * owner], order[2 * owner + 1]
    return jnp.where(at < BLK, low * BLK + at, (high - 1) * BLK + at)


def prob_body(heads, scale, order, who, q, g, k, k_far, prob, near, far):
    rows, hd = k.shape
    all_keys = jnp.concatenate([k[...], k_far[...]], axis=0)
    mine = places(order, who[0], (rows, rows), 0)
    here = places(order, who[0], (rows, rows), 1)
    back = places(order, who[1], (rows, rows), 1)
    allowed = jnp.concatenate([here <= mine, back <= mine], axis=1)
    total = jnp.zeros((2 * rows, hd), F32)
    for h in range(heads):
        cols = slice(h * hd, (h + 1) * hd)
        scores = jnp.where(allowed, dot(q[:, cols], all_keys, 1, 1) * scale, -1e30)
        weights = jnp.exp(scores - jnp.max(scores, axis=1, keepdims=True))
        p = (weights * (1.0 / jnp.sum(weights, axis=1, keepdims=True))).astype(BF)
        prob[h] = p
        total += dot(p, g[:, cols], 0, 0)
    near[...] = total[:rows]
    far[...] = total[rows:].astype(BF)


def back_body(heads, scale, prob, q, g, k, k_far, v, v_far, attn, dq, near, far):
    rows, hd = k.shape
    all_keys = jnp.concatenate([k[...], k_far[...]], axis=0)
    all_values = jnp.concatenate([v[...], v_far[...]], axis=0)
    total = jnp.zeros((2 * rows, hd), F32)
    for h in range(heads):
        cols = slice(h * hd, (h + 1) * hd)
        p = prob[h]
        gh = g[:, cols]
        out = dot(p, all_values, 1, 0).astype(BF)
        attn[:, cols] = out
        delta = jnp.sum(gh.astype(F32) * out.astype(F32), axis=1, keepdims=True)
        ds = (p.astype(F32) * (dot(gh, all_values, 1, 1) - delta)).astype(BF)
        dq[:, cols] = (dot(ds, all_keys, 1, 0) * scale).astype(BF)
        total += dot(ds, q[:, cols], 0, 0)
    near[...] = total[:rows] * scale
    far[...] = (total[rows:] * scale).astype(BF)


def term_body(part, who, x, near, back, mine, theirs):
    dv = (near[...] + back[...].astype(F32)).astype(BF)
    first = who[2] == 0
    group = NC * NX * part
    step = 2 * group
    for j in range(x.shape[1] // step):
        t = dot(x[:, j * step : (j + 1) * step], dv, 0, 0)
        at = slice(2 * part * j, 2 * part * (j + 1))
        for quarter in range(NX):

            def rows_of(c):
                low = c * NX * part + quarter * part
                return jnp.concatenate([t[low : low + part], t[group + low : group + low + part]], axis=0)

            zero, one = rows_of(0), rows_of(1)
            mine[quarter, at] = jnp.where(first, zero, one).astype(BF)
            theirs[quarter, at] = jnp.where(first, one, zero).astype(BF)


def quarter_of(who, step, mine, theirs):
    at = lax.rem(who[3] + step, NX)
    return mine[at].astype(F32) + theirs[at].astype(F32)


def far_body(who, mine, theirs, low, high):
    half = low.shape[0]
    far = quarter_of(who, 2, mine, theirs).astype(BF)
    low[...] = far[:half]
    high[...] = far[half:]


def side_body(who, mine, theirs, low, high, right, left):
    half = low.shape[0]
    one = quarter_of(who, 1, mine, theirs)
    right[:half] = (one[:half] + low[...].astype(F32)).astype(BF)
    right[half:] = one[half:].astype(BF)
    one = quarter_of(who, 3, mine, theirs)
    left[:half] = one[:half].astype(BF)
    left[half:] = (one[half:] + high[...].astype(F32)).astype(BF)


def own_body(who, mine, theirs, right, left, out):
    total = quarter_of(who, 0, mine, theirs) + right[...].astype(F32) + left[...].astype(F32)
    out[...] = total.astype(BF)


def sum_body(copies, parts, out):
    total = parts[0].astype(F32)
    for i in range(1, parts.shape[0]):
        total += parts[i].astype(F32)
    total = total.astype(BF)
    if copies == 0:
        out[...] = total
    else:
        for i in range(copies):
            out[:, i] = total


def summed(parts, copies):
    shape = parts.shape[1:]
    if copies:
        shape = (shape[0], copies) + shape[1:]
    out = jax.ShapeDtypeStruct(shape, BF)
    return kernel(functools.partial(sum_body, copies), [VM], [out], parts.size)(parts)[0]


def gathered_weight(w):
    def everywhere(block, axis):
        count = lax.axis_size(axis)
        return exchanged(jnp.broadcast_to(block[None], (count,) + block.shape), axis)

    own = everywhere(w, "zl")
    mine = everywhere(own, "y").reshape((NY * NZ,) + w.shape)
    theirs = shifted(mine, "c", 1)
    first = lax.axis_index("c") == 0
    both = jnp.stack([jnp.where(first, mine, theirs), jnp.where(first, theirs, mine)], axis=1)
    return both.reshape(NY * NZ * NC * w.shape[0], w.shape[1])


def scattered_sum(who, x_rows, near, back, part):
    rows, width = x_rows.shape
    hd = near.shape[1]
    full = (NX, NY * NZ * part, hd)
    mine, theirs = kernel(
        functools.partial(term_body, part),
        [SM, VM, VM, VM],
        [jax.ShapeDtypeStruct(full, BF)] * 2,
        2 * rows * width * hd,
    )(who, x_rows, near, back)
    theirs = shifted(theirs, "c", 1)
    size = NY * NZ * part
    quarter = jax.ShapeDtypeStruct((size, hd), BF)
    half = jax.ShapeDtypeStruct((size // 2, hd), BF)
    low, high = kernel(far_body, [SM, VM, VM], [half] * 2, size * hd)(who, mine, theirs)
    low = shifted(low, "x", 1)
    high = shifted(high, "x", -1)
    right, left = kernel(side_body, [SM] + [VM] * 4, [quarter] * 2, 2 * size * hd)(who, mine, theirs, low, high)
    right = shifted(right, "x", 1)
    left = shifted(left, "x", -1)
    total = kernel(own_body, [SM] + [VM] * 4, [quarter], size * hd)(who, mine, theirs, right, left)[0]
    total = total.reshape(NY, NZ, part, hd)
    got = exchanged(total, "y")
    total = summed(got, NH).reshape(NZ * NH, part, hd)
    got = exchanged(total, ("zl", "zh"))
    total = summed(got[:, None], NX)[0]
    return exchanged(total, "x").reshape(NX * part, hd).astype(F32)


def shards(inputs, block_order, w_value, query, keys, out_grad):
    x_rows = inputs[0]
    q_rows = query[0]
    k_rows = keys[0]
    grad_rows = out_grad[0]
    rows, hd = k_rows.shape
    heads = q_rows.shape[1] // hd
    scale = 1.0 / hd**0.5
    index = lax.axis_index(CTX)
    count = lax.axis_size(CTX)
    who = jnp.stack([index, (index + count - 1) % count, lax.axis_index("c"), lax.axis_index("x")]).astype(jnp.int32)
    block = jax.ShapeDtypeStruct((rows, hd), F32)
    block_b = jax.ShapeDtypeStruct((rows, hd), BF)
    wide_b = jax.ShapeDtypeStruct(q_rows.shape, BF)
    work = 2 * rows * 2 * rows * hd * heads

    far_keys = shifted(k_rows, CTX, 1)
    w_full = gathered_weight(w_value)

    prob, near, far = kernel(
        functools.partial(prob_body, heads, scale),
        [SM, SM, VM, VM, VM, VM],
        [jax.ShapeDtypeStruct((heads, rows, 2 * rows), BF), block, block_b],
        4 * work,
    )(in_hbm(block_order), who, in_hbm(q_rows), in_hbm(grad_rows), in_hbm(k_rows), far_keys)
    back = shifted(far, CTX, -1)
    grad_w = scattered_sum(who, x_rows, near, back, w_value.shape[0] // NX)

    values = jnp.dot(x_rows, w_full, preferred_element_type=F32).astype(BF)
    far_values = shifted(values, CTX, 1)
    attn, dquery, near_k, far_k = kernel(
        functools.partial(back_body, heads, scale),
        [VM] * 7,
        [wide_b, wide_b, block, block_b],
        6 * work,
    )(prob, q_rows, grad_rows, k_rows, far_keys, values, far_values)
    back_keys = shifted(far_k, CTX, -1).astype(F32)
    dkeys = (near_k + back_keys).astype(BF)
    return (attn[None], dquery[None], dkeys[None], grad_w)


def solution(mesh):
    fine = Mesh(mesh.devices.reshape(NY, NZ, NC, NX, NH), ("y", "zl", "c", "x", "zh"))
    return jax.shard_map(
        shards,
        mesh=fine,
        in_specs=(
            P(DP, CTX, None),
            P(),
            P(DP, None),
            P(DP, CTX, None),
            P(DP, CTX, None),
            P(DP, CTX, None),
        ),
        out_specs=(P(DP, CTX, None), P(DP, CTX, None), P(DP, CTX, None), P(DP, None)),
        check_vma=False,
    )
```

time: 177 us -> 162 us (0.915)
  local copies, waits for them, and re-layouts: 32.3 us -> 4.43 us
  blocking collectives: 0 us -> 22.4 us
  Pallas kernels: 0 us -> 12.6 us
  other arithmetic: 14.6 us -> 3.33 us
  matrix products: 11.9 us -> 0.76 us
  waiting for transfers between devices: 30.8 us -> 36.6 us
  starting transfers between devices: 84.5 us -> 79.9 us
    all_to_all x0 -> x1, blocking collectives: none -> 22.4 us  [exchanged(): return lax.all_to_all(value, axis, 0, 0, tiled=True)]
    pallas_call x0 -> x8, Pallas kernels: none -> 12.6 us  [the longest x1 3.11 us: shards(): kernel(functools.partial(prob_body, heads, scale), [SM, SM, VM, VM, VM, V...]
    dot_general x7 -> x0, matrix products: 11.1 us -> none  [the longest x1 3.68 us: shards(): term = jnp.dot(x_rows.T, dvalues, preferred_element_type=F32)]
    ppermute x10, waiting for transfers between devices: 15.2 us -> 25.7 us  [shifted(): return lax.ppermute(value, axis, pairs)]
    all_to_all x5 -> x4, starting transfers between devices: 38.9 us -> 29 us  [exchanged(): return lax.all_to_all(value, axis, 0, 0, tiled=True)]
    another operation x5 -> x0, local copies, waits for them, and re-layouts: 7.44 us -> none  [the longest x2 4.12 us: shards(): g_flat = grad_rows.reshape(rows * head_count, head_size)]
    dot_general x1 -> x0, local copies, waits for them, and re-layouts: 6.04 us -> none  [shards(): term = jnp.dot(x_rows.T, dvalues, preferred_element_type=F32)]
    ppermute x10, starting transfers between devices: 45.6 us -> 50.9 us  [shifted(): return lax.ppermute(value, axis, pairs)]
  transfers between devices with their start and end apart: 15 -> 14, of which waited for: 7 -> 9; matrix products, arithmetic and copies ran while one was open for 32% -> 2% of each run, Pallas kernels for 0% -> 8%
where the time goes in v2:
time: 162 us; the launch traced here: 161 us
  starting transfers between devices  79.9 us (49%)
  waiting for transfers between devices  36.6 us (23%)
  blocking collectives  22.4 us (14%)
  Pallas kernels  12.6 us (8%)
  local copies, waits for them, and re-layouts  4.43 us (3%)
  other arithmetic  3.33 us (2%)
    ppermute x10, starting transfers between devices, shifted(): return lax.ppermute(value, axis, pairs)  50.9 us
    all_to_all x4, starting transfers between devices, exchanged(): return lax.all_to_all(value, axis, 0, 0, tiled=True)  29 us
    ppermute x10, waiting for transfers between devices, shifted(): return lax.ppermute(value, axis, pairs)  25.7 us
    all_to_all x1, blocking collectives, exchanged(): return lax.all_to_all(value, axis, 0, 0, tiled=True)  22.4 us
    all_to_all x4, waiting for transfers between devices, exchanged(): return lax.all_to_all(value, axis, 0, 0, tiled=True)  10.9 us
  transfers between devices with their start and end apart: 14, of which 9 were waited for; matrix products, arithmetic and copies ran while one was open for 2% of the time, Pallas kernels for 8%

profile of v2, /device:TPU:2, one launch (start us, length us, event | category | flops | bytes accessed | tf_op | source)
XLA Modules:
  0.0 160.9 jit_solution(10845849362450973609)
XLA Ops:
  1.4 22.4 %all_to_all.25 = bf16[6,96,128]{2,1,0:T(8,128)(2,1)S(1)} all-to-all(bf16[6,96,128]{2,1,0:T(8,128)(2,1)S(1)} %broadcast_in_dim.24), channel_id=1, replica_groups=mesh['y'=8,'zl'=6,'c'=2,'x'=4,'zh'=2] {'zl'}, dimensions={0} | all-to-all | bytes 294912 | tf_op jit(solution)/shard_map/all_to_all | solution.py:32
  25.0 7.2 %all-to-all-start.1 = ((bf16[8,6,96,128]{3,2,1,0:T(8,128)(2,1)}), bf16[8,6,96,128]{3,2,1,0:T(8,128)(2,1)}, u32[]{:S(2)}, u32[]{:S(2)}) async-start(bf16[8,6,96,128]{3,2,1,0:T(8,128)(2,1)} %broadcast_in_dim.25), calls=%async_computation.1 | async-start | bytes 2359296 | tf_op jit(solution)/shard_map/all_to_all | solution.py:32
  32.2 10.0 %collective-permute-start = (bf16[128,128]{1,0:T(8,128)(2,1)S(1)}, bf16[128,128]{1,0:T(8,128)(2,1)S(1)}, u32[]{:S(2)}, u32[]{:S(2)}) collective-permute-start(bf16[128,128]{1,0:T(8,128)(2,1)S(1)} %bitcast.41), channel_id=1, source_target_pairs={{0,1},{1,2},{2,3},{3,4},{4,5},{5,6},{6,7},{7,0},{8,9},{9,10},{10,1... | collective-permute-start | bytes 98312 | tf_op jit(solution)/shard_map/ppermute | solution.py:28
  42.4 3.4 %collective-permute-done.k_far = bf16[128,128]{1,0:T(8,128)(2,1)S(1)} collective-permute-done((bf16[128,128]{1,0:T(8,128)(2,1)S(1)}, bf16[128,128]{1,0:T(8,128)(2,1)S(1)}, u32[]{:S(2)}, u32[]{:S(2)}) %collective-permute-start) | collective-permute-done | bytes 32800 | tf_op jit(solution)/shard_map/ppermute | solution.py:28
  45.7 3.1 %shard_map.93 = (bf16[16,128,256]{2,1,0:T(8,128)(2,1)S(1)}, f32[128,128]{1,0:T(8,128)S(1)}, bf16[128,128]{1,0:T(8,128)(2,1)S(1)}) custom-call(s32[16]{0:T(128)} %order.1, s32[4]{0:T(128)S(1)} %pad_add_fusion.who, bf16[128,2048]{1,0:T(8,128)(2,1)} %bitcast.36, bf16[128,2048]{1,0:T(8,128)(2,1)} %bitcast.38, bf16[128,128]{1,0:T(8,128)(2,1)} %bitcast.40, ...), custom_call_target="tpu_custom_call" | custom-call | flops 536870912 | bytes 2293760 | tf_op jit(solution)/shard_map/pallas_call | solution.py:222
  49.8 8.6 %collective-permute-start.4 = (bf16[128,128]{1,0:T(8,128)(2,1)S(1)}, bf16[128,128]{1,0:T(8,128)(2,1)S(1)}, u32[]{:S(2)}, u32[]{:S(2)}) collective-permute-start(bf16[128,128]{1,0:T(8,128)(2,1)S(1)} %get-tuple-element.23), channel_id=1, source_target_pairs={{0,7},{1,0},{2,1},{3,2},{4,3},{5,4},{6,5},{7,6},{8,15},{9,8},{10,9... | collective-permute-start | bytes 98312 | tf_op jit(solution)/shard_map/ppermute | solution.py:28
  58.4 3.5 %collective-permute-done.4.back = bf16[128,128]{1,0:T(8,128)(2,1)S(1)} collective-permute-done((bf16[128,128]{1,0:T(8,128)(2,1)S(1)}, bf16[128,128]{1,0:T(8,128)(2,1)S(1)}, u32[]{:S(2)}, u32[]{:S(2)}) %collective-permute-start.4) | collective-permute-done | bytes 32800 | tf_op jit(solution)/shard_map/ppermute | solution.py:28
  61.9 2.4 %shard_map.95 = (bf16[4,1152,128]{2,1,0:T(8,128)(2,1)S(1)}, bf16[4,1152,128]{2,1,0:T(8,128)(2,1)}) custom-call(s32[4]{0:T(128)S(1)} %pad_add_fusion.who, bf16[128,9216]{1,0:T(8,128)(2,1)S(1)} %bitcast.34, f32[128,128]{1,0:T(8,128)S(1)} %get-tuple-element.22.near, bf16[128,128]{1,0:T(8,128)(2,1)S(1)} %collective-permute-done.4.back), custom_call_target="tpu_custom_call" | custom-call | flops 301989888 | bytes 4718592 | tf_op jit(solution)/shard_map/pallas_call | solution.py:178
  66.3 2.4 %collective-permute-start.1 = (bf16[48,96,128]{2,1,0:T(8,128)(2,1)}, bf16[48,96,128]{2,1,0:T(8,128)(2,1)}, u32[]{:S(2)}, u32[]{:S(2)}) collective-permute-start(bf16[48,96,128]{2,1,0:T(8,128)(2,1)} %bitcast.7), channel_id=1, source_target_pairs={{0,8},{8,0},{1,9},{9,1},{2,10},{10,2},{3,11},{11,3},{4,12},{12,4},... | collective-permute-start | bytes 3538952 | tf_op jit(solution)/shard_map/ppermute | solution.py:28
  69.9 3.4 %collective-permute-start.6 = (bf16[576,128]{1,0:T(8,128)(2,1)S(1)}, bf16[576,128]{1,0:T(8,128)(2,1)S(1)}, u32[]{:S(2)}, u32[]{:S(2)}) collective-permute-start(bf16[576,128]{1,0:T(8,128)(2,1)S(1)} %get-tuple-element.26), channel_id=1, source_target_pairs={{0,2},{2,4},{4,6},{6,0},{1,3},{3,5},{5,7},{7,1},{8,10},{10,12},{12... | collective-permute-start | bytes 442376 | tf_op jit(solution)/shard_map/ppermute | solution.py:28
  73.3 2.4 %collective-permute-start.7 = (bf16[576,128]{1,0:T(8,128)(2,1)S(1)}, bf16[576,128]{1,0:T(8,128)(2,1)S(1)}, u32[]{:S(2)}, u32[]{:S(2)}) collective-permute-start(bf16[576,128]{1,0:T(8,128)(2,1)S(1)} %get-tuple-element.27), channel_id=1, source_target_pairs={{0,6},{2,0},{4,2},{6,4},{1,7},{3,1},{5,3},{7,5},{8,14},{10,8},{12,... | collective-permute-start | bytes 442376 | tf_op jit(solution)/shard_map/ppermute | solution.py:28
  77.7 3.1 %collective-permute-done.7.high = bf16[576,128]{1,0:T(8,128)(2,1)S(1)} collective-permute-done((bf16[576,128]{1,0:T(8,128)(2,1)S(1)}, bf16[576,128]{1,0:T(8,128)(2,1)S(1)}, u32[]{:S(2)}, u32[]{:S(2)}) %collective-permute-start.7) | collective-permute-done | bytes 147488 | tf_op jit(solution)/shard_map/ppermute | solution.py:28
  81.6 3.3 %collective-permute-start.8 = (bf16[1152,128]{1,0:T(8,128)(2,1)S(1)}, bf16[1152,128]{1,0:T(8,128)(2,1)S(1)}, u32[]{:S(2)}, u32[]{:S(2)}) collective-permute-start(bf16[1152,128]{1,0:T(8,128)(2,1)S(1)} %get-tuple-element.28), channel_id=1, source_target_pairs={{0,2},{2,4},{4,6},{6,0},{1,3},{3,5},{5,7},{7,1},{8,10},{10,12},{12... | collective-permute-start | bytes 884744 | tf_op jit(solution)/shard_map/ppermute | solution.py:28
  84.9 2.5 %collective-permute-start.9 = (bf16[1152,128]{1,0:T(8,128)(2,1)S(1)}, bf16[1152,128]{1,0:T(8,128)(2,1)S(1)}, u32[]{:S(2)}, u32[]{:S(2)}) collective-permute-start(bf16[1152,128]{1,0:T(8,128)(2,1)S(1)} %get-tuple-element.29), channel_id=1, source_target_pairs={{0,6},{2,0},{4,2},{6,4},{1,7},{3,1},{5,3},{7,5},{8,14},{10,8},{12,... | collective-permute-start | bytes 884744 | tf_op jit(solution)/shard_map/ppermute | solution.py:28
  87.4 3.9 %collective-permute-done.8.right = bf16[1152,128]{1,0:T(8,128)(2,1)S(1)} collective-permute-done((bf16[1152,128]{1,0:T(8,128)(2,1)S(1)}, bf16[1152,128]{1,0:T(8,128)(2,1)S(1)}, u32[]{:S(2)}, u32[]{:S(2)}) %collective-permute-start.8) | collective-permute-done | bytes 294944 | tf_op jit(solution)/shard_map/ppermute | solution.py:28
  91.4 3.9 %collective-permute-done.9.left = bf16[1152,128]{1,0:T(8,128)(2,1)S(1)} collective-permute-done((bf16[1152,128]{1,0:T(8,128)(2,1)S(1)}, bf16[1152,128]{1,0:T(8,128)(2,1)S(1)}, u32[]{:S(2)}, u32[]{:S(2)}) %collective-permute-start.9) | collective-permute-done | bytes 294944 | tf_op jit(solution)/shard_map/ppermute | solution.py:28
  96.7 7.1 %all-to-all-start.2 = ((bf16[8,6,24,128]{3,2,1,0:T(8,128)(2,1)}), bf16[8,6,24,128]{3,2,1,0:T(8,128)(2,1)S(1)}, u32[]{:S(2)}, u32[]{:S(2)}) async-start(bf16[8,6,24,128]{3,2,1,0:T(8,128)(2,1)} %bitcast.17), calls=%async_computation.2 | async-start | bytes 589824 | tf_op jit(solution)/shard_map/all_to_all | solution.py:32
  103.7 10.9 %all-to-all-done.2.parts = bf16[8,6,24,128]{3,2,1,0:T(8,128)(2,1)S(1)} async-done(((bf16[8,6,24,128]{3,2,1,0:T(8,128)(2,1)}), bf16[8,6,24,128]{3,2,1,0:T(8,128)(2,1)S(1)}, u32[]{:S(2)}, u32[]{:S(2)}) %all-to-all-start.2) | async-done | bytes 294944 | tf_op jit(solution)/shard_map/all_to_all | solution.py:32
  115.3 9.3 %all-to-all-start.3 = ((bf16[12,24,128]{2,1,0:T(8,128)(2,1)}), bf16[12,24,128]{2,1,0:T(8,128)(2,1)S(1)}, u32[]{:S(2)}, u32[]{:S(2)}) async-start(bf16[12,24,128]{2,1,0:T(8,128)(2,1)} %bitcast.18), calls=%async_computation.3 | async-start | bytes 147456 | tf_op jit(solution)/shard_map/all_to_all | solution.py:32
  128.8 10.2 %collective-permute-start.2 = (bf16[128,128]{1,0:T(8,128)(2,1)S(1)}, bf16[128,128]{1,0:T(8,128)(2,1)S(1)}, u32[]{:S(2)}, u32[]{:S(2)}) collective-permute-start(bf16[128,128]{1,0:T(8,128)(2,1)S(1)} %fusion.v), channel_id=1, source_target_pairs={{0,1},{1,2},{2,3},{3,4},{4,5},{5,6},{6,7},{7,0},{8,9},{9,10},{10,1... | collective-permute-start | bytes 98312 | tf_op jit(solution)/shard_map/ppermute | solution.py:28
  139.7 5.4 %all-to-all-start.4 = ((bf16[4,24,128]{2,1,0:T(8,128)(2,1)}), bf16[4,24,128]{2,1,0:T(8,128)(2,1)S(1)}, u32[]{:S(2)}, u32[]{:S(2)}) async-start(bf16[4,24,128]{2,1,0:T(8,128)(2,1)} %bitcast.20), calls=%async_computation.4 | async-start | bytes 49152 | tf_op jit(solution)/shard_map/all_to_all | solution.py:32
  145.1 3.0 %shard_map.94 = (bf16[128,2048]{1,0:T(8,128)(2,1)}, bf16[128,2048]{1,0:T(8,128)(2,1)}, f32[128,128]{1,0:T(8,128)S(1)}, bf16[128,128]{1,0:T(8,128)(2,1)S(1)}) custom-call(bf16[16,128,256]{2,1,0:T(8,128)(2,1)S(1)} %copy-done.9, bf16[128,2048]{1,0:T(8,128)(2,1)S(1)} %bitcast.37, bf16[128,2048]{1,0:T(8,128)(2,1)S(1)} %bitcast.39, bf16[128,128]{1,0:T(8,128)(2,1)S(1)} %bitcast.42, ...), custom_call_target="tpu_custom_call" | custom-call | flops 805306368 | bytes 2293760 | tf_op jit(solution)/shard_map/pallas_call | solution.py:233
  148.1 6.0 %collective-permute-start.3 = (bf16[128,128]{1,0:T(8,128)(2,1)S(1)}, bf16[128,128]{1,0:T(8,128)(2,1)S(1)}, u32[]{:S(2)}, u32[]{:S(2)}) collective-permute-start(bf16[128,128]{1,0:T(8,128)(2,1)S(1)} %get-tuple-element.21), channel_id=1, source_target_pairs={{0,7},{1,0},{2,1},{3,2},{4,3},{5,4},{6,5},{7,6},{8,15},{9,8},{10,9... | collective-permute-start | bytes 98312 | tf_op jit(solution)/shard_map/ppermute | solution.py:28
  154.8 5.4 %collective-permute-done.3 = bf16[128,128]{1,0:T(8,128)(2,1)S(1)} collective-permute-done((bf16[128,128]{1,0:T(8,128)(2,1)S(1)}, bf16[128,128]{1,0:T(8,128)(2,1)S(1)}, u32[]{:S(2)}, u32[]{:S(2)}) %collective-permute-start.3) | collective-permute-done | bytes 32800 | tf_op jit(solution)/shard_map/ppermute | solution.py:28
  (41 shorter events, 17.0 us)
Async XLA Ops:
  23.8 8.5 %copy-start.4 = (bf16[1,128,128]{2,1,0:T(8,128)(2,1)S(1)}, bf16[1,128,128]{2,1,0:T(8,128)(2,1)}, u32[]{:S(2)}) copy-start(bf16[1,128,128]{2,1,0:T(8,128)(2,1)} %param.10) | copy-start | bytes 98308
  25.0 36.9 %copy-start = (bf16[1,128,9216]{2,1,0:T(8,128)(2,1)S(1)}, bf16[1,128,9216]{2,1,0:T(8,128)(2,1)}, u32[]{:S(2)}) copy-start(bf16[1,128,9216]{2,1,0:T(8,128)(2,1)} %param.6) | copy-start | bytes 7077892
  25.0 41.3 %all-to-all-start.1 = ((bf16[8,6,96,128]{3,2,1,0:T(8,128)(2,1)}), bf16[8,6,96,128]{3,2,1,0:T(8,128)(2,1)}, u32[]{:S(2)}, u32[]{:S(2)}) async-start(bf16[8,6,96,128]{3,2,1,0:T(8,128)(2,1)} %broadcast_in_dim.25), calls=%async_computation.1 | async-start | bytes 2359296 | tf_op jit(solution)/shard_map/all_to_all | solution.py:32
  32.2 13.5 %collective-permute-start = (bf16[128,128]{1,0:T(8,128)(2,1)S(1)}, bf16[128,128]{1,0:T(8,128)(2,1)S(1)}, u32[]{:S(2)}, u32[]{:S(2)}) collective-permute-start(bf16[128,128]{1,0:T(8,128)(2,1)S(1)} %bitcast.41), channel_id=1, source_target_pairs={{0,1},{1,2},{2,3},{3,4},{4,5},{5,6},{6,7},{7,0},{8,9},{9,10},{10,1... | collective-permute-start | bytes 98312 | tf_op jit(solution)/shard_map/ppermute | solution.py:28
  45.7 16.2 %copy-start.6 = (bf16[128,128]{1,0:T(8,128)(2,1)}, bf16[128,128]{1,0:T(8,128)(2,1)S(1)}, u32[]{:S(2)}) copy-start(bf16[128,128]{1,0:T(8,128)(2,1)S(1)} %collective-permute-done.k_far) | copy-start | bytes 98308
  48.9 1.0 copy-start.8
  49.8 12.1 %collective-permute-start.4 = (bf16[128,128]{1,0:T(8,128)(2,1)S(1)}, bf16[128,128]{1,0:T(8,128)(2,1)S(1)}, u32[]{:S(2)}, u32[]{:S(2)}) collective-permute-start(bf16[128,128]{1,0:T(8,128)(2,1)S(1)} %get-tuple-element.23), channel_id=1, source_target_pairs={{0,7},{1,0},{2,1},{3,2},{4,3},{5,4},{6,5},{7,6},{8,15},{9,8},{10,9... | collective-permute-start | bytes 98312 | tf_op jit(solution)/shard_map/ppermute | solution.py:28
  64.3 4.9 %collective-permute-start.5 = (bf16[4,1152,128]{2,1,0:T(8,128)(2,1)}, bf16[4,1152,128]{2,1,0:T(8,128)(2,1)S(1)}, u32[]{:S(2)}, u32[]{:S(2)}) collective-permute-start(bf16[4,1152,128]{2,1,0:T(8,128)(2,1)} %get-tuple-element.25), channel_id=1, source_target_pairs={{0,8},{8,0},{1,9},{9,1},{2,10},{10,2},{3,11},{11,3},{4,12},{12,4},... | collective-permute-start | bytes 3538952 | tf_op jit(solution)/shard_map/ppermute | solution.py:28
  66.3 58.3 %collective-permute-start.1 = (bf16[48,96,128]{2,1,0:T(8,128)(2,1)}, bf16[48,96,128]{2,1,0:T(8,128)(2,1)}, u32[]{:S(2)}, u32[]{:S(2)}) collective-permute-start(bf16[48,96,128]{2,1,0:T(8,128)(2,1)} %bitcast.7), channel_id=1, source_target_pairs={{0,8},{8,0},{1,9},{9,1},{2,10},{10,2},{3,11},{11,3},{4,12},{12,4},... | collective-permute-start | bytes 3538952 | tf_op jit(solution)/shard_map/ppermute | solution.py:28
  69.9 7.8 %collective-permute-start.6 = (bf16[576,128]{1,0:T(8,128)(2,1)S(1)}, bf16[576,128]{1,0:T(8,128)(2,1)S(1)}, u32[]{:S(2)}, u32[]{:S(2)}) collective-permute-start(bf16[576,128]{1,0:T(8,128)(2,1)S(1)} %get-tuple-element.26), channel_id=1, source_target_pairs={{0,2},{2,4},{4,6},{6,0},{1,3},{3,5},{5,7},{7,1},{8,10},{10,12},{12... | collective-permute-start | bytes 442376 | tf_op jit(solution)/shard_map/ppermute | solution.py:28
  73.3 7.5 %collective-permute-start.7 = (bf16[576,128]{1,0:T(8,128)(2,1)S(1)}, bf16[576,128]{1,0:T(8,128)(2,1)S(1)}, u32[]{:S(2)}, u32[]{:S(2)}) collective-permute-start(bf16[576,128]{1,0:T(8,128)(2,1)S(1)} %get-tuple-element.27), channel_id=1, source_target_pairs={{0,6},{2,0},{4,2},{6,4},{1,7},{3,1},{5,3},{7,5},{8,14},{10,8},{12,... | collective-permute-start | bytes 442376 | tf_op jit(solution)/shard_map/ppermute | solution.py:28
  81.6 9.8 %collective-permute-start.8 = (bf16[1152,128]{1,0:T(8,128)(2,1)S(1)}, bf16[1152,128]{1,0:T(8,128)(2,1)S(1)}, u32[]{:S(2)}, u32[]{:S(2)}) collective-permute-start(bf16[1152,128]{1,0:T(8,128)(2,1)S(1)} %get-tuple-element.28), channel_id=1, source_target_pairs={{0,2},{2,4},{4,6},{6,0},{1,3},{3,5},{5,7},{7,1},{8,10},{10,12},{12... | collective-permute-start | bytes 884744 | tf_op jit(solution)/shard_map/ppermute | solution.py:28
  84.9 10.3 %collective-permute-start.9 = (bf16[1152,128]{1,0:T(8,128)(2,1)S(1)}, bf16[1152,128]{1,0:T(8,128)(2,1)S(1)}, u32[]{:S(2)}, u32[]{:S(2)}) collective-permute-start(bf16[1152,128]{1,0:T(8,128)(2,1)S(1)} %get-tuple-element.29), channel_id=1, source_target_pairs={{0,6},{2,0},{4,2},{6,4},{1,7},{3,1},{5,3},{7,5},{8,14},{10,8},{12,... | collective-permute-start | bytes 884744 | tf_op jit(solution)/shard_map/ppermute | solution.py:28
  96.7 18.0 %all-to-all-start.2 = ((bf16[8,6,24,128]{3,2,1,0:T(8,128)(2,1)}), bf16[8,6,24,128]{3,2,1,0:T(8,128)(2,1)S(1)}, u32[]{:S(2)}, u32[]{:S(2)}) async-start(bf16[8,6,24,128]{3,2,1,0:T(8,128)(2,1)} %bitcast.17), calls=%async_computation.2 | async-start | bytes 589824 | tf_op jit(solution)/shard_map/all_to_all | solution.py:32
  115.3 23.7 %all-to-all-start.3 = ((bf16[12,24,128]{2,1,0:T(8,128)(2,1)}), bf16[12,24,128]{2,1,0:T(8,128)(2,1)S(1)}, u32[]{:S(2)}, u32[]{:S(2)}) async-start(bf16[12,24,128]{2,1,0:T(8,128)(2,1)} %bitcast.18), calls=%async_computation.3 | async-start | bytes 147456 | tf_op jit(solution)/shard_map/all_to_all | solution.py:32
  126.4 1.7 %copy-start.1 = (bf16[1,128,9216]{2,1,0:T(8,128)(2,1)S(1)}, bf16[1,128,9216]{2,1,0:T(8,128)(2,1)}, u32[]{:S(2)}) copy-start(bf16[1,128,9216]{2,1,0:T(8,128)(2,1)} %param.6) | copy-start | bytes 7077892
  128.0 17.1 %copy-start.2 = (bf16[1,128,2048]{2,1,0:T(8,128)(2,1)S(1)}, bf16[1,128,2048]{2,1,0:T(8,128)(2,1)}, u32[]{:S(2)}) copy-start(bf16[1,128,2048]{2,1,0:T(8,128)(2,1)} %param.9) | copy-start | bytes 1572868
  128.0 17.1 %copy-start.3 = (bf16[1,128,2048]{2,1,0:T(8,128)(2,1)S(1)}, bf16[1,128,2048]{2,1,0:T(8,128)(2,1)}, u32[]{:S(2)}) copy-start(bf16[1,128,2048]{2,1,0:T(8,128)(2,1)} %param.11) | copy-start | bytes 1572868
  128.0 17.1 %copy-start.5 = (bf16[1,128,128]{2,1,0:T(8,128)(2,1)S(1)}, bf16[1,128,128]{2,1,0:T(8,128)(2,1)}, u32[]{:S(2)}) copy-start(bf16[1,128,128]{2,1,0:T(8,128)(2,1)} %param.10) | copy-start | bytes 98308
  128.0 17.1 %copy-start.7 = (bf16[128,128]{1,0:T(8,128)(2,1)S(1)}, bf16[128,128]{1,0:T(8,128)(2,1)}, u32[]{:S(2)}) copy-start(bf16[128,128]{1,0:T(8,128)(2,1)} %copy-done.6) | copy-start | bytes 98308
  128.0 17.1 %copy-start.9 = (bf16[16,128,256]{2,1,0:T(8,128)(2,1)S(1)}, bf16[16,128,256]{2,1,0:T(8,128)(2,1)}, u32[]{:S(2)}) copy-start(bf16[16,128,256]{2,1,0:T(8,128)(2,1)} %copy-done.8) | copy-start | bytes 3145732
  128.8 16.3 %collective-permute-start.2 = (bf16[128,128]{1,0:T(8,128)(2,1)S(1)}, bf16[128,128]{1,0:T(8,128)(2,1)S(1)}, u32[]{:S(2)}, u32[]{:S(2)}) collective-permute-start(bf16[128,128]{1,0:T(8,128)(2,1)S(1)} %fusion.v), channel_id=1, source_target_pairs={{0,1},{1,2},{2,3},{3,4},{4,5},{5,6},{6,7},{7,0},{8,9},{9,10},{10,1... | collective-permute-start | bytes 98312 | tf_op jit(solution)/shard_map/ppermute | solution.py:28
  139.7 14.5 %all-to-all-start.4 = ((bf16[4,24,128]{2,1,0:T(8,128)(2,1)}), bf16[4,24,128]{2,1,0:T(8,128)(2,1)S(1)}, u32[]{:S(2)}, u32[]{:S(2)}) async-start(bf16[4,24,128]{2,1,0:T(8,128)(2,1)} %bitcast.20), calls=%async_computation.4 | async-start | bytes 49152 | tf_op jit(solution)/shard_map/all_to_all | solution.py:32
  148.1 12.1 %collective-permute-start.3 = (bf16[128,128]{1,0:T(8,128)(2,1)S(1)}, bf16[128,128]{1,0:T(8,128)(2,1)S(1)}, u32[]{:S(2)}, u32[]{:S(2)}) collective-permute-start(bf16[128,128]{1,0:T(8,128)(2,1)S(1)} %get-tuple-element.21), channel_id=1, source_target_pairs={{0,7},{1,0},{2,1},{3,2},{4,3},{5,4},{6,5},{7,6},{8,15},{9,8},{10,9... | collective-permute-start | bytes 98312 | tf_op jit(solution)/shard_map/ppermute | solution.py:28

commit v3 on v2

--- a/solution.py
+++ b/solution.py
@@ -32,7 +32,7 @@
     return lax.all_to_all(value, axis, 0, 0, tiled=True)
 
 
-def kernel(body, ins, outs, flops, limit=24 * 2**20):
+def kernel(body, ins, outs, flops):
     size = sum(o.size * o.dtype.itemsize for o in outs)
     return pl.pallas_call(
         body,
@@ -40,7 +40,7 @@
         in_specs=ins,
         out_specs=[VM] * len(outs),
         cost_estimate=pl.CostEstimate(flops=flops, bytes_accessed=2 * size, transcendentals=0),
-        compiler_params=pltpu.CompilerParams(vmem_limit_bytes=limit),
+        compiler_params=pltpu.CompilerParams(vmem_limit_bytes=24 * 2**20),
     )
 
 
@@ -54,21 +54,36 @@
     return jnp.where(at < BLK, low * BLK + at, (high - 1) * BLK + at)
 
 
-def prob_body(heads, scale, order, who, q, g, k, k_far, prob, near, far):
-    rows, hd = k.shape
+def probabilities(scale, order, who, k, k_far):
+    rows = k.shape[0]
     all_keys = jnp.concatenate([k[...], k_far[...]], axis=0)
     mine = places(order, who[0], (rows, rows), 0)
     here = places(order, who[0], (rows, rows), 1)
     back = places(order, who[1], (rows, rows), 1)
     allowed = jnp.concatenate([here <= mine, back <= mine], axis=1)
+
+    def of(q):
+        scores = jnp.where(allowed, dot(q, all_keys, 1, 1) * scale, -1e30)
+        weights = jnp.exp(scores - jnp.max(scores, axis=1, keepdims=True))
+        return (weights * (1.0 / jnp.sum(weights, axis=1, keepdims=True))).astype(BF)
+
+    return of
+
+
+def prob_body(heads, scale, order, who, q, k, k_far, prob):
+    hd = k.shape[1]
+    of = probabilities(scale, order, who, k, k_far)
+    for h in range(heads):
+        prob[h] = of(q[:, h * hd : (h + 1) * hd])
+
+
+def dval_body(heads, scale, order, who, q, g, k, k_far, near, far):
+    rows, hd = k.shape
+    of = probabilities(scale, order, who, k, k_far)
     total = jnp.zeros((2 * rows, hd), F32)
     for h in range(heads):
         cols = slice(h * hd, (h + 1) * hd)
-        scores = jnp.where(allowed, dot(q[:, cols], all_keys, 1, 1) * scale, -1e30)
-        weights = jnp.exp(scores - jnp.max(scores, axis=1, keepdims=True))
-        p = (weights * (1.0 / jnp.sum(weights, axis=1, keepdims=True))).astype(BF)
-        prob[h] = p
-        total += dot(p, g[:, cols], 0, 0)
+        total += dot(of(q[:, cols]), g[:, cols], 0, 0)
     near[...] = total[:rows]
     far[...] = total[rows:].astype(BF)
 
@@ -116,33 +131,23 @@
     return mine[at].astype(F32) + theirs[at].astype(F32)
 
 
-def far_body(who, mine, theirs, low, high):
-    half = low.shape[0]
-    far = quarter_of(who, 2, mine, theirs).astype(BF)
-    low[...] = far[:half]
-    high[...] = far[half:]
-
-
-def side_body(who, mine, theirs, low, high, right, left):
-    half = low.shape[0]
-    one = quarter_of(who, 1, mine, theirs)
-    right[:half] = (one[:half] + low[...].astype(F32)).astype(BF)
-    right[half:] = one[half:].astype(BF)
-    one = quarter_of(who, 3, mine, theirs)
-    left[:half] = one[:half].astype(BF)
-    left[half:] = (one[half:] + high[...].astype(F32)).astype(BF)
-
-
-def own_body(who, mine, theirs, right, left, out):
-    total = quarter_of(who, 0, mine, theirs) + right[...].astype(F32) + left[...].astype(F32)
-    out[...] = total.astype(BF)
+def sides_body(who, mine, theirs, *outs):
+    for step, out in enumerate(outs, 1):
+        out[...] = quarter_of(who, step, mine, theirs).astype(BF)
+
+
+def own_body(who, mine, theirs, *refs):
+    total = quarter_of(who, 0, mine, theirs)
+    for ref in refs[:-1]:
+        total += ref[...].astype(F32)
+    refs[-1][...] = total.astype(BF)
 
 
 def sum_body(copies, parts, out):
     total = parts[0].astype(F32)
     for i in range(1, parts.shape[0]):
         total += parts[i].astype(F32)
-    total = total.astype(BF)
+    total = total.astype(out.dtype)
     if copies == 0:
         out[...] = total
     else:
@@ -150,11 +155,11 @@
             out[:, i] = total
 
 
-def summed(parts, copies):
+def summed(parts, copies, kind=BF):
     shape = parts.shape[1:]
     if copies:
         shape = (shape[0], copies) + shape[1:]
-    out = jax.ShapeDtypeStruct(shape, BF)
+    out = jax.ShapeDtypeStruct(shape, kind)
     return kernel(functools.partial(sum_body, copies), [VM], [out], parts.size)(parts)[0]
 
 
@@ -184,20 +189,17 @@
     theirs = shifted(theirs, "c", 1)
     size = NY * NZ * part
     quarter = jax.ShapeDtypeStruct((size, hd), BF)
-    half = jax.ShapeDtypeStruct((size // 2, hd), BF)
-    low, high = kernel(far_body, [SM, VM, VM], [half] * 2, size * hd)(who, mine, theirs)
-    low = shifted(low, "x", 1)
-    high = shifted(high, "x", -1)
-    right, left = kernel(side_body, [SM] + [VM] * 4, [quarter] * 2, 2 * size * hd)(who, mine, theirs, low, high)
-    right = shifted(right, "x", 1)
-    left = shifted(left, "x", -1)
-    total = kernel(own_body, [SM] + [VM] * 4, [quarter], size * hd)(who, mine, theirs, right, left)[0]
+    sides = kernel(sides_body, [SM, VM, VM], [quarter] * 3, 3 * size * hd)(who, mine, theirs)
+    got = []
+    for step, side in zip((2, 1, 3), (sides[1], sides[0], sides[2])):
+        got.append(shifted(side, "x", step))
+    total = kernel(own_body, [SM] + [VM] * 5, [quarter], size * hd)(who, mine, theirs, *got)[0]
     total = total.reshape(NY, NZ, part, hd)
     got = exchanged(total, "y")
     total = summed(got, NH).reshape(NZ * NH, part, hd)
     got = exchanged(total, ("zl", "zh"))
-    total = summed(got[:, None], NX)[0]
-    return exchanged(total, "x").reshape(NX * part, hd).astype(F32)
+    total = summed(got[:, None], NX, F32)[0]
+    return exchanged(total, "x").reshape(NX * part, hd)
 
 
 def shards(inputs, block_order, w_value, query, keys, out_grad):
@@ -219,12 +221,15 @@
     far_keys = shifted(k_rows, CTX, 1)
     w_full = gathered_weight(w_value)
 
-    prob, near, far = kernel(
+    near, far = kernel(
+        functools.partial(dval_body, heads, scale), [SM, SM] + [VM] * 4, [block, block_b], 4 * work
+    )(in_hbm(block_order), who, in_hbm(q_rows), in_hbm(grad_rows), in_hbm(k_rows), far_keys)
+    prob = kernel(
         functools.partial(prob_body, heads, scale),
-        [SM, SM, VM, VM, VM, VM],
-        [jax.ShapeDtypeStruct((heads, rows, 2 * rows), BF), block, block_b],
-        4 * work,
-    )(in_hbm(block_order), who, in_hbm(q_rows), in_hbm(grad_rows), in_hbm(k_rows), far_keys)
+        [SM, SM] + [VM] * 3,
+        [jax.ShapeDtypeStruct((heads, rows, 2 * rows), BF)],
+        2 * work,
+    )(in_hbm(block_order), who, in_hbm(q_rows), in_hbm(k_rows), in_hbm(far_keys))[0]
     back = shifted(far, CTX, -1)
     grad_w = scattered_sum(who, x_rows, near, back, w_value.shape[0] // NX)
 
@@ -235,7 +240,7 @@
         [VM] * 7,
         [wide_b, wide_b, block, block_b],
         6 * work,
-    )(prob, q_rows, grad_rows, k_rows, far_keys, values, far_values)
+    )(in_hbm(prob), in_hbm(q_rows), in_hbm(grad_rows), k_rows, far_keys, values, far_values)
     back_keys = shifted(far_k, CTX, -1).astype(F32)
     dkeys = (near_k + back_keys).astype(BF)
     return (attn[None], dquery[None], dkeys[None], grad_w)

time: 162 us -> 161 us (level)
  Pallas kernels: 12.6 us -> 16.2 us
  starting transfers between devices: 79.9 us -> 76.5 us
    ppermute x10 -> x9, starting transfers between devices: 50.9 us -> 47.7 us  [shifted(): return lax.ppermute(value, axis, pairs)]
    pallas_call x4, Pallas kernels: 5.89 us -> 8.07 us  [the longest x1 3.11 us: shards(): kernel(functools.partial(dval_body, heads, scale), [SM, SM] + [VM] * 4, [...]
    ppermute x10 -> x9, waiting for transfers between devices: 25.7 us -> 24 us  [shifted(): return lax.ppermute(value, axis, pairs)]
  transfers between devices with their start and end apart: 14 -> 13, of which waited for: 9 -> 7; matrix products, arithmetic and copies ran while one was open for 2% -> 2% of each run, Pallas kernels for 8% -> 10%
where the time goes in v3:
time: 161 us; the launch traced here: 160 us
  starting transfers between devices  76.5 us (48%)
  waiting for transfers between devices  36.5 us (23%)
  blocking collectives  22.4 us (14%)
  Pallas kernels  16.2 us (10%)
  local copies, waits for them, and re-layouts  4.34 us (3%)
  other arithmetic  2.7 us (2%)
    ppermute x9, starting transfers between devices, shifted(): return lax.ppermute(value, axis, pairs)  47.7 us
    all_to_all x4, starting transfers between devices, exchanged(): return lax.all_to_all(value, axis, 0, 0, tiled=True)  28.9 us
    ppermute x9, waiting for transfers between devices, shifted(): return lax.ppermute(value, axis, pairs)  24 us
    all_to_all x1, blocking collectives, exchanged(): return lax.all_to_all(value, axis, 0, 0, tiled=True)  22.4 us
    all_to_all x4, waiting for transfers between devices, exchanged(): return lax.all_to_all(value, axis, 0, 0, tiled=True)  12.5 us
    pallas_call x1, Pallas kernels, shards(): kernel(functools.partial(back_body, heads, scale), [VM] * 7, [wide_b, wid...  4.46 us
  transfers between devices with their start and end apart: 13, of which 7 were waited for; matrix products, arithmetic and copies ran while one was open for 2% of the time, Pallas kernels for 10%

profile of v3, /device:TPU:2, one launch (start us, length us, event | category | flops | bytes accessed | tf_op | source)
XLA Modules:
  0.0 160.3 jit_solution(17713771554873546376)
XLA Ops:
  1.4 22.4 %all_to_all.25 = bf16[6,96,128]{2,1,0:T(8,128)(2,1)S(1)} all-to-all(bf16[6,96,128]{2,1,0:T(8,128)(2,1)S(1)} %broadcast_in_dim.24), channel_id=1, replica_groups=mesh['y'=8,'zl'=6,'c'=2,'x'=4,'zh'=2] {'zl'}, dimensions={0} | all-to-all | bytes 294912 | tf_op jit(solution)/shard_map/all_to_all | solution.py:32
  25.0 7.2 %all-to-all-start.1 = ((bf16[8,6,96,128]{3,2,1,0:T(8,128)(2,1)}), bf16[8,6,96,128]{3,2,1,0:T(8,128)(2,1)}, u32[]{:S(2)}, u32[]{:S(2)}) async-start(bf16[8,6,96,128]{3,2,1,0:T(8,128)(2,1)} %broadcast_in_dim.25), calls=%async_computation.1 | async-start | bytes 2359296 | tf_op jit(solution)/shard_map/all_to_all | solution.py:32
  32.2 10.0 %collective-permute-start = (bf16[128,128]{1,0:T(8,128)(2,1)S(1)}, bf16[128,128]{1,0:T(8,128)(2,1)S(1)}, u32[]{:S(2)}, u32[]{:S(2)}) collective-permute-start(bf16[128,128]{1,0:T(8,128)(2,1)S(1)} %bitcast.37), channel_id=1, source_target_pairs={{0,1},{1,2},{2,3},{3,4},{4,5},{5,6},{6,7},{7,0},{8,9},{9,10},{10,1... | collective-permute-start | bytes 98312 | tf_op jit(solution)/shard_map/ppermute | solution.py:28
  42.4 3.4 %collective-permute-done.k_far = bf16[128,128]{1,0:T(8,128)(2,1)S(1)} collective-permute-done((bf16[128,128]{1,0:T(8,128)(2,1)S(1)}, bf16[128,128]{1,0:T(8,128)(2,1)S(1)}, u32[]{:S(2)}, u32[]{:S(2)}) %collective-permute-start) | collective-permute-done | bytes 32800 | tf_op jit(solution)/shard_map/ppermute | solution.py:28
  45.7 3.1 %shard_map.95 = (f32[128,128]{1,0:T(8,128)S(1)}, bf16[128,128]{1,0:T(8,128)(2,1)S(1)}) custom-call(s32[16]{0:T(128)} %order.3, s32[4]{0:T(128)S(1)} %pad_add_fusion.who, bf16[128,2048]{1,0:T(8,128)(2,1)} %bitcast.40, bf16[128,2048]{1,0:T(8,128)(2,1)} %bitcast.44, bf16[128,128]{1,0:T(8,128)(2,1)} %bitcast.35, bf16[128,128]{1,0:T(8,128)(2,1)S(1)} %collective-permute-done.k_far), custom_call_target="tpu_custom_call" | custom-call | flops 536870912 | bytes 196608 | tf_op jit(solution)/shard_map/pallas_call | solution.py:224
  48.8 8.6 %collective-permute-start.4 = (bf16[128,128]{1,0:T(8,128)(2,1)S(1)}, bf16[128,128]{1,0:T(8,128)(2,1)S(1)}, u32[]{:S(2)}, u32[]{:S(2)}) collective-permute-start(bf16[128,128]{1,0:T(8,128)(2,1)S(1)} %get-tuple-element.20), channel_id=1, source_target_pairs={{0,7},{1,0},{2,1},{3,2},{4,3},{5,4},{6,5},{7,6},{8,15},{9,8},{10,9... | collective-permute-start | bytes 98312 | tf_op jit(solution)/shard_map/ppermute | solution.py:28
  57.5 3.5 %collective-permute-done.4.back = bf16[128,128]{1,0:T(8,128)(2,1)S(1)} collective-permute-done((bf16[128,128]{1,0:T(8,128)(2,1)S(1)}, bf16[128,128]{1,0:T(8,128)(2,1)S(1)}, u32[]{:S(2)}, u32[]{:S(2)}) %collective-permute-start.4) | collective-permute-done | bytes 32800 | tf_op jit(solution)/shard_map/ppermute | solution.py:28
  61.0 2.4 %shard_map.96 = (bf16[4,1152,128]{2,1,0:T(8,128)(2,1)S(1)}, bf16[4,1152,128]{2,1,0:T(8,128)(2,1)}) custom-call(s32[4]{0:T(128)S(1)} %pad_add_fusion.who, bf16[128,9216]{1,0:T(8,128)(2,1)S(1)} %bitcast.32, f32[128,128]{1,0:T(8,128)S(1)} %get-tuple-element.19.near, bf16[128,128]{1,0:T(8,128)(2,1)S(1)} %collective-permute-done.4.back), custom_call_target="tpu_custom_call" | custom-call | flops 301989888 | bytes 4718592 | tf_op jit(solution)/shard_map/pallas_call | solution.py:183
  63.4 1.9 %collective-permute-start.5 = (bf16[4,1152,128]{2,1,0:T(8,128)(2,1)}, bf16[4,1152,128]{2,1,0:T(8,128)(2,1)}, u32[]{:S(2)}, u32[]{:S(2)}) collective-permute-start(bf16[4,1152,128]{2,1,0:T(8,128)(2,1)} %get-tuple-element.22), channel_id=1, source_target_pairs={{0,8},{8,0},{1,9},{9,1},{2,10},{10,2},{3,11},{11,3},{4,12},{12,4},... | collective-permute-start | bytes 3538952 | tf_op jit(solution)/shard_map/ppermute | solution.py:28
  65.3 2.4 %collective-permute-start.1 = (bf16[48,96,128]{2,1,0:T(8,128)(2,1)}, bf16[48,96,128]{2,1,0:T(8,128)(2,1)}, u32[]{:S(2)}, u32[]{:S(2)}) collective-permute-start(bf16[48,96,128]{2,1,0:T(8,128)(2,1)} %bitcast.7), channel_id=1, source_target_pairs={{0,8},{8,0},{1,9},{9,1},{2,10},{10,2},{3,11},{11,3},{4,12},{12,4},... | collective-permute-start | bytes 3538952 | tf_op jit(solution)/shard_map/ppermute | solution.py:28
  69.9 4.3 %collective-permute-start.6 = (bf16[1152,128]{1,0:T(8,128)(2,1)S(1)}, bf16[1152,128]{1,0:T(8,128)(2,1)S(1)}, u32[]{:S(2)}, u32[]{:S(2)}) collective-permute-start(bf16[1152,128]{1,0:T(8,128)(2,1)S(1)} %get-tuple-element.23), channel_id=1, source_target_pairs={{0,4},{2,6},{4,0},{6,2},{1,5},{3,7},{5,1},{7,3},{8,12},{10,14},{12... | collective-permute-start | bytes 884744 | tf_op jit(solution)/shard_map/ppermute | solution.py:28
  74.2 2.7 %collective-permute-start.7 = (bf16[1152,128]{1,0:T(8,128)(2,1)S(1)}, bf16[1152,128]{1,0:T(8,128)(2,1)S(1)}, u32[]{:S(2)}, u32[]{:S(2)}) collective-permute-start(bf16[1152,128]{1,0:T(8,128)(2,1)S(1)} %get-tuple-element.24), channel_id=1, source_target_pairs={{0,2},{2,4},{4,6},{6,0},{1,3},{3,5},{5,7},{7,1},{8,10},{10,12},{12... | collective-permute-start | bytes 884744 | tf_op jit(solution)/shard_map/ppermute | solution.py:28
  76.9 3.2 %collective-permute-start.8 = (bf16[1152,128]{1,0:T(8,128)(2,1)S(1)}, bf16[1152,128]{1,0:T(8,128)(2,1)S(1)}, u32[]{:S(2)}, u32[]{:S(2)}) collective-permute-start(bf16[1152,128]{1,0:T(8,128)(2,1)S(1)} %get-tuple-element.25), channel_id=1, source_target_pairs={{0,6},{2,0},{4,2},{6,4},{1,7},{3,1},{5,3},{7,5},{8,14},{10,8},{12,... | collective-permute-start | bytes 884744 | tf_op jit(solution)/shard_map/ppermute | solution.py:28
  80.0 3.0 %collective-permute-done.6.refs_0_ = bf16[1152,128]{1,0:T(8,128)(2,1)S(1)} collective-permute-done((bf16[1152,128]{1,0:T(8,128)(2,1)S(1)}, bf16[1152,128]{1,0:T(8,128)(2,1)S(1)}, u32[]{:S(2)}, u32[]{:S(2)}) %collective-permute-start.6) | collective-permute-done | bytes 294944 | tf_op jit(solution)/shard_map/ppermute | solution.py:28
  83.0 5.8 %collective-permute-done.7.refs_1_ = bf16[1152,128]{1,0:T(8,128)(2,1)S(1)} collective-permute-done((bf16[1152,128]{1,0:T(8,128)(2,1)S(1)}, bf16[1152,128]{1,0:T(8,128)(2,1)S(1)}, u32[]{:S(2)}, u32[]{:S(2)}) %collective-permute-start.7) | collective-permute-done | bytes 294944 | tf_op jit(solution)/shard_map/ppermute | solution.py:28
  91.0 7.1 %all-to-all-start.2 = ((bf16[8,6,24,128]{3,2,1,0:T(8,128)(2,1)}), bf16[8,6,24,128]{3,2,1,0:T(8,128)(2,1)S(1)}, u32[]{:S(2)}, u32[]{:S(2)}) async-start(bf16[8,6,24,128]{3,2,1,0:T(8,128)(2,1)} %bitcast.33), calls=%async_computation.2 | async-start | bytes 589824 | tf_op jit(solution)/shard_map/all_to_all | solution.py:32
  98.0 12.5 %all-to-all-done.2.parts = bf16[8,6,24,128]{3,2,1,0:T(8,128)(2,1)S(1)} async-done(((bf16[8,6,24,128]{3,2,1,0:T(8,128)(2,1)}), bf16[8,6,24,128]{3,2,1,0:T(8,128)(2,1)S(1)}, u32[]{:S(2)}, u32[]{:S(2)}) %all-to-all-start.2) | async-done | bytes 294944 | tf_op jit(solution)/shard_map/all_to_all | solution.py:32
  111.2 9.1 %all-to-all-start.3 = ((bf16[12,24,128]{2,1,0:T(8,128)(2,1)}), bf16[12,24,128]{2,1,0:T(8,128)(2,1)S(1)}, u32[]{:S(2)}, u32[]{:S(2)}) async-start(bf16[12,24,128]{2,1,0:T(8,128)(2,1)} %bitcast.18), calls=%async_computation.3 | async-start | bytes 147456 | tf_op jit(solution)/shard_map/all_to_all | solution.py:32
  123.1 10.2 %collective-permute-start.2 = (bf16[128,128]{1,0:T(8,128)(2,1)S(1)}, bf16[128,128]{1,0:T(8,128)(2,1)S(1)}, u32[]{:S(2)}, u32[]{:S(2)}) collective-permute-start(bf16[128,128]{1,0:T(8,128)(2,1)S(1)} %fusion.v), channel_id=1, source_target_pairs={{0,1},{1,2},{2,3},{3,4},{4,5},{5,6},{6,7},{7,0},{8,9},{9,10},{10,1... | collective-permute-start | bytes 98312 | tf_op jit(solution)/shard_map/ppermute | solution.py:28
  133.3 2.0 %shard_map.93.prob = bf16[16,128,256]{2,1,0:T(8,128)(2,1)S(1)} custom-call(s32[16]{0:T(128)} %order.3, s32[4]{0:T(128)S(1)} %pad_add_fusion.who, bf16[128,2048]{1,0:T(8,128)(2,1)} %bitcast.41, bf16[128,128]{1,0:T(8,128)(2,1)} %bitcast.36, bf16[128,128]{1,0:T(8,128)(2,1)} %copy-done.5), custom_call_target="tpu_custom_call" | custom-call | flops 268435456 | bytes 2097152 | tf_op jit(solution)/shard_map/pallas_call | solution.py:227
  137.0 5.5 %all-to-all-start.4 = ((f32[4,24,128]{2,1,0:T(8,128)}), f32[4,24,128]{2,1,0:T(8,128)S(1)}, u32[]{:S(2)}, u32[]{:S(2)}) async-start(f32[4,24,128]{2,1,0:T(8,128)} %bitcast.20), calls=%async_computation.4 | async-start | bytes 98304 | tf_op jit(solution)/shard_map/all_to_all | solution.py:32
  142.5 4.5 %shard_map.94 = (bf16[128,2048]{1,0:T(8,128)(2,1)}, bf16[128,2048]{1,0:T(8,128)(2,1)}, f32[128,128]{1,0:T(8,128)S(1)}, bf16[128,128]{1,0:T(8,128)(2,1)S(1)}) custom-call(bf16[16,128,256]{2,1,0:T(8,128)(2,1)} %copy-done.2, bf16[128,2048]{1,0:T(8,128)(2,1)} %bitcast.42, bf16[128,2048]{1,0:T(8,128)(2,1)} %bitcast.45, bf16[128,128]{1,0:T(8,128)(2,1)S(1)} %bitcast.38, ...), custom_call_target="tpu_custom_call" | custom-call | flops 805306368 | bytes 2293760 | tf_op jit(solution)/shard_map/pallas_call | solution.py:238
  147.0 4.4 %collective-permute-start.3 = (bf16[128,128]{1,0:T(8,128)(2,1)S(1)}, bf16[128,128]{1,0:T(8,128)(2,1)S(1)}, u32[]{:S(2)}, u32[]{:S(2)}) collective-permute-start(bf16[128,128]{1,0:T(8,128)(2,1)S(1)} %get-tuple-element.18), channel_id=1, source_target_pairs={{0,7},{1,0},{2,1},{3,2},{4,3},{5,4},{6,5},{7,6},{8,15},{9,8},{10,9... | collective-permute-start | bytes 98312 | tf_op jit(solution)/shard_map/ppermute | solution.py:28
  151.4 7.7 %collective-permute-done.3 = bf16[128,128]{1,0:T(8,128)(2,1)S(1)} collective-permute-done((bf16[128,128]{1,0:T(8,128)(2,1)S(1)}, bf16[128,128]{1,0:T(8,128)(2,1)S(1)}, u32[]{:S(2)}, u32[]{:S(2)}) %collective-permute-start.3) | collective-permute-done | bytes 32800 | tf_op jit(solution)/shard_map/ppermute | solution.py:28
  (33 shorter events, 12.9 us)
Async XLA Ops:
  23.8 8.5 %copy-start.3 = (bf16[1,128,128]{2,1,0:T(8,128)(2,1)S(1)}, bf16[1,128,128]{2,1,0:T(8,128)(2,1)}, u32[]{:S(2)}) copy-start(bf16[1,128,128]{2,1,0:T(8,128)(2,1)} %param.10) | copy-start | bytes 98308
  25.0 36.0 %copy-start = (bf16[1,128,9216]{2,1,0:T(8,128)(2,1)S(1)}, bf16[1,128,9216]{2,1,0:T(8,128)(2,1)}, u32[]{:S(2)}) copy-start(bf16[1,128,9216]{2,1,0:T(8,128)(2,1)} %param.6) | copy-start | bytes 7077892
  25.0 40.3 %all-to-all-start.1 = ((bf16[8,6,96,128]{3,2,1,0:T(8,128)(2,1)}), bf16[8,6,96,128]{3,2,1,0:T(8,128)(2,1)}, u32[]{:S(2)}, u32[]{:S(2)}) async-start(bf16[8,6,96,128]{3,2,1,0:T(8,128)(2,1)} %broadcast_in_dim.25), calls=%async_computation.1 | async-start | bytes 2359296 | tf_op jit(solution)/shard_map/all_to_all | solution.py:32
  32.2 13.5 %collective-permute-start = (bf16[128,128]{1,0:T(8,128)(2,1)S(1)}, bf16[128,128]{1,0:T(8,128)(2,1)S(1)}, u32[]{:S(2)}, u32[]{:S(2)}) collective-permute-start(bf16[128,128]{1,0:T(8,128)(2,1)S(1)} %bitcast.37), channel_id=1, source_target_pairs={{0,1},{1,2},{2,3},{3,4},{4,5},{5,6},{6,7},{7,0},{8,9},{9,10},{10,1... | collective-permute-start | bytes 98312 | tf_op jit(solution)/shard_map/ppermute | solution.py:28
  45.7 15.2 %copy-start.5 = (bf16[128,128]{1,0:T(8,128)(2,1)}, bf16[128,128]{1,0:T(8,128)(2,1)S(1)}, u32[]{:S(2)}) copy-start(bf16[128,128]{1,0:T(8,128)(2,1)S(1)} %collective-permute-done.k_far) | copy-start | bytes 98308
  48.8 12.1 %collective-permute-start.4 = (bf16[128,128]{1,0:T(8,128)(2,1)S(1)}, bf16[128,128]{1,0:T(8,128)(2,1)S(1)}, u32[]{:S(2)}, u32[]{:S(2)}) collective-permute-start(bf16[128,128]{1,0:T(8,128)(2,1)S(1)} %get-tuple-element.20), channel_id=1, source_target_pairs={{0,7},{1,0},{2,1},{3,2},{4,3},{5,4},{6,5},{7,6},{8,15},{9,8},{10,9... | collective-permute-start | bytes 98312 | tf_op jit(solution)/shard_map/ppermute | solution.py:28
  63.4 5.1 %collective-permute-start.5 = (bf16[4,1152,128]{2,1,0:T(8,128)(2,1)}, bf16[4,1152,128]{2,1,0:T(8,128)(2,1)}, u32[]{:S(2)}, u32[]{:S(2)}) collective-permute-start(bf16[4,1152,128]{2,1,0:T(8,128)(2,1)} %get-tuple-element.22), channel_id=1, source_target_pairs={{0,8},{8,0},{1,9},{9,1},{2,10},{10,2},{3,11},{11,3},{4,12},{12,4},... | collective-permute-start | bytes 3538952 | tf_op jit(solution)/shard_map/ppermute | solution.py:28
  65.3 55.0 %collective-permute-start.1 = (bf16[48,96,128]{2,1,0:T(8,128)(2,1)}, bf16[48,96,128]{2,1,0:T(8,128)(2,1)}, u32[]{:S(2)}, u32[]{:S(2)}) collective-permute-start(bf16[48,96,128]{2,1,0:T(8,128)(2,1)} %bitcast.7), channel_id=1, source_target_pairs={{0,8},{8,0},{1,9},{9,1},{2,10},{10,2},{3,11},{11,3},{4,12},{12,4},... | collective-permute-start | bytes 3538952 | tf_op jit(solution)/shard_map/ppermute | solution.py:28
  69.9 13.1 %collective-permute-start.6 = (bf16[1152,128]{1,0:T(8,128)(2,1)S(1)}, bf16[1152,128]{1,0:T(8,128)(2,1)S(1)}, u32[]{:S(2)}, u32[]{:S(2)}) collective-permute-start(bf16[1152,128]{1,0:T(8,128)(2,1)S(1)} %get-tuple-element.23), channel_id=1, source_target_pairs={{0,4},{2,6},{4,0},{6,2},{1,5},{3,7},{5,1},{7,3},{8,12},{10,14},{12... | collective-permute-start | bytes 884744 | tf_op jit(solution)/shard_map/ppermute | solution.py:28
  74.2 14.6 %collective-permute-start.7 = (bf16[1152,128]{1,0:T(8,128)(2,1)S(1)}, bf16[1152,128]{1,0:T(8,128)(2,1)S(1)}, u32[]{:S(2)}, u32[]{:S(2)}) collective-permute-start(bf16[1152,128]{1,0:T(8,128)(2,1)S(1)} %get-tuple-element.24), channel_id=1, source_target_pairs={{0,2},{2,4},{4,6},{6,0},{1,3},{3,5},{5,7},{7,1},{8,10},{10,12},{12... | collective-permute-start | bytes 884744 | tf_op jit(solution)/shard_map/ppermute | solution.py:28
  76.9 11.9 %collective-permute-start.8 = (bf16[1152,128]{1,0:T(8,128)(2,1)S(1)}, bf16[1152,128]{1,0:T(8,128)(2,1)S(1)}, u32[]{:S(2)}, u32[]{:S(2)}) collective-permute-start(bf16[1152,128]{1,0:T(8,128)(2,1)S(1)} %get-tuple-element.25), channel_id=1, source_target_pairs={{0,6},{2,0},{4,2},{6,4},{1,7},{3,1},{5,3},{7,5},{8,14},{10,8},{12,... | collective-permute-start | bytes 884744 | tf_op jit(solution)/shard_map/ppermute | solution.py:28
  90.3 0.7 copy-start.1
  91.0 19.5 %all-to-all-start.2 = ((bf16[8,6,24,128]{3,2,1,0:T(8,128)(2,1)}), bf16[8,6,24,128]{3,2,1,0:T(8,128)(2,1)S(1)}, u32[]{:S(2)}, u32[]{:S(2)}) async-start(bf16[8,6,24,128]{3,2,1,0:T(8,128)(2,1)} %bitcast.33), calls=%async_computation.2 | async-start | bytes 589824 | tf_op jit(solution)/shard_map/all_to_all | solution.py:32
  111.2 25.2 %all-to-all-start.3 = ((bf16[12,24,128]{2,1,0:T(8,128)(2,1)}), bf16[12,24,128]{2,1,0:T(8,128)(2,1)S(1)}, u32[]{:S(2)}, u32[]{:S(2)}) async-start(bf16[12,24,128]{2,1,0:T(8,128)(2,1)} %bitcast.18), calls=%async_computation.3 | async-start | bytes 147456 | tf_op jit(solution)/shard_map/all_to_all | solution.py:32
  123.1 19.4 %copy-start.4 = (bf16[1,128,128]{2,1,0:T(8,128)(2,1)S(1)}, bf16[1,128,128]{2,1,0:T(8,128)(2,1)}, u32[]{:S(2)}) copy-start(bf16[1,128,128]{2,1,0:T(8,128)(2,1)} %param.10) | copy-start | bytes 98308
  123.1 19.4 %copy-start.6 = (bf16[128,128]{1,0:T(8,128)(2,1)S(1)}, bf16[128,128]{1,0:T(8,128)(2,1)}, u32[]{:S(2)}) copy-start(bf16[128,128]{1,0:T(8,128)(2,1)} %copy-done.5) | copy-start | bytes 98308
  123.1 19.4 %collective-permute-start.2 = (bf16[128,128]{1,0:T(8,128)(2,1)S(1)}, bf16[128,128]{1,0:T(8,128)(2,1)S(1)}, u32[]{:S(2)}, u32[]{:S(2)}) collective-permute-start(bf16[128,128]{1,0:T(8,128)(2,1)S(1)} %fusion.v), channel_id=1, source_target_pairs={{0,1},{1,2},{2,3},{3,4},{4,5},{5,6},{6,7},{7,0},{8,9},{9,10},{10,1... | collective-permute-start | bytes 98312 | tf_op jit(solution)/shard_map/ppermute | solution.py:28
  135.3 1.0 copy-start.2
  137.0 14.4 %all-to-all-start.4 = ((f32[4,24,128]{2,1,0:T(8,128)}), f32[4,24,128]{2,1,0:T(8,128)S(1)}, u32[]{:S(2)}, u32[]{:S(2)}) async-start(f32[4,24,128]{2,1,0:T(8,128)} %bitcast.20), calls=%async_computation.4 | async-start | bytes 98304 | tf_op jit(solution)/shard_map/all_to_all | solution.py:32
  147.0 12.1 %collective-permute-start.3 = (bf16[128,128]{1,0:T(8,128)(2,1)S(1)}, bf16[128,128]{1,0:T(8,128)(2,1)S(1)}, u32[]{:S(2)}, u32[]{:S(2)}) collective-permute-start(bf16[128,128]{1,0:T(8,128)(2,1)S(1)} %get-tuple-element.18), channel_id=1, source_target_pairs={{0,7},{1,0},{2,1},{3,2},{4,3},{5,4},{6,5},{7,6},{8,15},{9,8},{10,9... | collective-permute-start | bytes 98312 | tf_op jit(solution)/shard_map/ppermute | solution.py:28
